TPU v7x, 128 devices: a whole 4x4x4 slice. The times are simulated.
128 devices in a mesh: row: 8 (over z_hi, y), col: 16 (over z_lo, x, core).
Axes of the slice: x: 4, y: 4, z: 4 (z_hi: 2, z_lo: 2; z = z_hi * 2 + z_lo), core: 2. Of those that a mesh axis runs over, the one named last changes fastest.
Arguments:
- object_field: float32 [2, 4096, 8192], P(None, 'row', 'col'), may hold values from -5 to 5
- probe: float32 [2, 8, 256, 256], replicated, may hold values from -2.5 to 2.5
- intensity: float32 [256, 256, 256], P(('row', 'col')), may hold values from 0.5 to 4
- row_offset: int32 [256], P(('row', 'col')), may hold values from 0 to 511
- col_offset: int32 [256], P(('row', 'col')), may hold values from 0 to 511
- live: int32 [256], P(('row', 'col')), may hold values 0 or 1
Outputs:
- object_grad: float32 [2, 4096, 8192], P(None, 'row', 'col')
- probe_grad: float32 [2, 8, 256, 256], replicated
All inputs are finite; a program needn't handle non-finite values. No bound on the sum of `live` on one device may be relied on, other than what follows from the above.
Results may differ from a plain program's by a relative error of at most 0.0003.
Values sent between devices are 32-bit elements; how exact they have to be, the bound alone decides.
A program may use at most 128 MiB of HBM per device.

v0:
```python
import jax
import jax.numpy as jnp
from jax import lax
from jax.sharding import PartitionSpec as P

smoothing = 0.25


def passed_along(array, axis, by):
    devices = lax.axis_size(axis)
    pairs = [(i, i + by) for i in range(devices) if 0 <= i + by < devices]
    return lax.ppermute(array, axis, pairs)


def tables(width):
    index = jnp.arange(width, dtype=jnp.int32)
    product = index[:, None] * index[None, :] % width
    phase = product.astype(jnp.float32) * (2.0 * jnp.pi / width)
    scale = 1.0 / jnp.sqrt(jnp.float32(width))
    return (jnp.cos(phase) * scale, jnp.sin(phase) * scale)


def transform(field_re, field_im, cosine, sine):
    best = lax.Precision.HIGHEST
    left_re = jnp.einsum("ab,pmbc->pmac", cosine, field_re, precision=best) + jnp.einsum(
        "ab,pmbc->pmac", sine, field_im, precision=best
    )
    left_im = jnp.einsum("ab,pmbc->pmac", cosine, field_im, precision=best) - jnp.einsum(
        "ab,pmbc->pmac", sine, field_re, precision=best
    )
    out_re = jnp.einsum("pmac,cd->pmad", left_re, cosine, precision=best) + jnp.einsum(
        "pmac,cd->pmad", left_im, sine, precision=best
    )
    out_im = jnp.einsum("pmac,cd->pmad", left_im, cosine, precision=best) - jnp.einsum(
        "pmac,cd->pmad", left_re, sine, precision=best
    )
    return (out_re, out_im)


def shards(object_field, probe, intensity, row_offset, col_offset, live):
    width = probe.shape[-1]
    tile_rows = object_field.shape[1]
    tile_cols = object_field.shape[2]
    right_part = passed_along(object_field, "col", -1)
    upper = jnp.concatenate([object_field, right_part], axis=2)
    lower_part = passed_along(upper, "row", -1)
    extended = jnp.concatenate([upper, lower_part], axis=1)
    anchor = jnp.zeros((), jnp.int32)

    def take_patch(top, left):
        return lax.dynamic_slice(extended, (anchor, top, left), (2, width, width))

    patches = jax.vmap(take_patch)(row_offset, col_offset)
    patch_re = patches[:, 0][:, None]
    patch_im = patches[:, 1][:, None]
    probe_re = probe[0][None]
    probe_im = probe[1][None]
    exit_re = probe_re * patch_re - probe_im * patch_im
    exit_im = probe_re * patch_im + probe_im * patch_re
    cosine, sine = tables(width)
    spec_re, spec_im = transform(exit_re, exit_im, cosine, sine)
    amplitude = jnp.sqrt(jnp.sum(spec_re * spec_re + spec_im * spec_im, axis=1) + smoothing)
    factor = (1.0 - jnp.sqrt(intensity) / amplitude) * live.astype(jnp.float32)[:, None, None]
    factor = factor[:, None]
    chi_re, chi_im = transform(spec_re * factor, spec_im * factor, cosine, -sine)
    partial_probe = jnp.stack(
        [
            jnp.sum(patch_re * chi_re + patch_im * chi_im, axis=0),
            jnp.sum(patch_re * chi_im - patch_im * chi_re, axis=0),
        ]
    )
    probe_grad = lax.psum(partial_probe, ("row", "col"))
    obj_re = jnp.sum(probe_re * chi_re + probe_im * chi_im, axis=1)
    obj_im = jnp.sum(probe_re * chi_im - probe_im * chi_re, axis=1)
    grad_ext = jnp.zeros_like(extended)
    for number in range(intensity.shape[0]):
        top = row_offset[number]
        left = col_offset[number]
        contrib = jnp.stack([obj_re[number], obj_im[number]])
        current = lax.dynamic_slice(grad_ext, (anchor, top, left), (2, width, width))
        grad_ext = lax.dynamic_update_slice(grad_ext, current + contrib, (anchor, top, left))
    lower_back = passed_along(grad_ext[:, tile_rows:, :], "row", 1)
    upper_grad = grad_ext[:, :tile_rows, :].at[:, :tile_rows, :].add(lower_back)
    right_back = passed_along(upper_grad[:, :, tile_cols:], "col", 1)
    object_grad = upper_grad[:, :, :tile_cols].at[:, :, :tile_cols].add(right_back)
    return (object_grad, probe_grad)


def solution(mesh):
    in_specs = (
        P(None, "row", "col"),
        P(),
        P(("row", "col"), None, None),
        P(("row", "col")),
        P(("row", "col")),
        P(("row", "col")),
    )
    out_specs = (P(None, "row", "col"), P())
    return jax.shard_map(shards, mesh=mesh, in_specs=in_specs, out_specs=out_specs, check_vma=False)
```

profile of v0, /device:TPU:1, one launch (start us, length us, event | category | flops | bytes accessed | tf_op | source)
XLA Modules:
  0.0 586.1 jit_solution(12317396587116852990)
XLA Ops:
  7.2 3.3 collective-permute-start
  13.6 22.4 %collective-permute-done = f32[2,512,512]{2,1,0:T(8,128)S(1)} collective-permute-done((f32[2,512,512]{2,1,0:T(8,128)}, f32[2,512,512]{2,1,0:T(8,128)S(1)}, u32[]{:S(2)}, u32[]{:S(2)}) %collective-permute-start) | collective-permute-done | bytes 2097184 | tf_op jit(solution)/shard_map/ppermute | solution.py:12
  47.9 3.9 slice_bitcast_fusion.1
  51.8 59.5 %collective-permute-done.1 = f32[2,512,1024]{2,1,0:T(8,128)} collective-permute-done((f32[2,512,1024]{2,1,0:T(8,128)}, f32[2,512,1024]{2,1,0:T(8,128)}, u32[]{:S(2)}, u32[]{:S(2)}) %collective-permute-start.1) | collective-permute-done | bytes 4194336 | tf_op jit(solution)/shard_map/ppermute | solution.py:12
  111.3 8.4 %pad_maximum_fusion = f32[2,1024,1024]{2,1,0:T(8,128)} fusion(f32[2,512,1024]{2,1,0:T(8,128)} %collective-permute-done.1, f32[2,512,1024]{2,1,0:T(8,128)} %constant_dynamic-update-slice_fusion), kind=kLoop, calls=%fused_computation.2 | loop fusion | flops 2097152 | bytes 16777216 | tf_op jit(solution)/shard_map/concatenate | solution.py:47
  119.7 7.2 %while.5 = (s32[]{:T(128)}, f32[2,1024,1024]{2,1,0:T(8,128)}, s32[2,3]{1,0:T(2,128)S(1)}, f32[2,2,256,256]{3,2,1,0:T(8,128)S(1)}, s32[]{:T(128)}) while((s32[]{:T(128)}, f32[2,1024,1024]{2,1,0:T(8,128)}, s32[2,3]{1,0:T(2,128)S(1)}, f32[2,2,256,256]{3,2,1,0:T(8,128)S(1)}, s32[]{:T(128)}) %tuple.50), condition=%wide.while_cond.2, body=%wide.while_body.2.sunk | while | flops 2 | bytes 1048693 | solution.py:51
  128.5 8.4 %fusion.17 = f32[2,8,256,256]{3,2,1,0:T(8,128)S(1)} fusion(f32[2,256,256]{2,1,0:T(8,128)S(1)} %get-tuple-element.73, f32[8,256,256]{2,1,0:T(8,128)S(1)} %copy-done, f32[2,256,256]{2,1,0:T(8,128)S(1)} %get-tuple-element.72, f32[8,256,256]{2,1,0:T(8,128)S(1)} %get-tuple-element.70), kind=kOutput, calls=%fused_computation.28 | convolution fusion | flops 3225354240 | bytes 9437184 | tf_op jit(solution)/shard_map/ab,pmbc->pmac/dot_general | solution.py:25
  136.9 8.5 %fusion.16 = f32[2,8,256,256]{3,2,1,0:T(8,128)S(1)} fusion(f32[2,256,256]{2,1,0:T(8,128)S(1)} %get-tuple-element.73, f32[8,256,256]{2,1,0:T(8,128)S(1)} %copy-done, f32[2,256,256]{2,1,0:T(8,128)S(1)} %get-tuple-element.72, f32[8,256,256]{2,1,0:T(8,128)S(1)} %get-tuple-element.70), kind=kOutput, calls=%fused_computation.27 | convolution fusion | flops 3225354240 | bytes 9437184 | tf_op jit(solution)/shard_map/ab,pmbc->pmac/dot_general | solution.py:28
  145.4 8.4 %fusion.55 = f32[2,8,256,256]{3,2,1,0:T(8,128)S(1)} fusion(f32[2,8,256,256]{3,2,1,0:T(8,128)S(1)} %fusion.16, f32[2,256,256]{2,1,0:T(8,128)S(1)} %get-tuple-element.73, f32[8,256,256]{2,1,0:T(8,128)S(1)} %copy-done, f32[2,256,256]{2,1,0:T(8,128)S(1)} %get-tuple-element.72, f32[8,256,256]{2,1,0:T(8,128)S(1)} %get-tuple-element.70), kind=kOutput, calls=%fused_computation.56 | convolution fusion | flops 3226402816 | bytes 13631488 | tf_op jit(solution)/shard_map/ab,pmbc->pmac/dot_general | solution.py:28
  153.8 8.4 %fusion.10 = f32[2,8,256,256]{3,2,1,0:T(8,128)S(1)} fusion(f32[2,8,256,256]{3,2,1,0:T(8,128)S(1)} %fusion.55), kind=kOutput, calls=%fused_computation.15 | convolution fusion | flops 3222208512 | bytes 8388608 | tf_op jit(solution)/shard_map/pmac,cd->pmad/dot_general | solution.py:31
  162.2 8.5 %fusion.8 = f32[2,8,256,256]{3,2,1,0:T(8,128)S(1)} fusion(f32[2,8,256,256]{3,2,1,0:T(8,128)S(1)} %fusion.55), kind=kOutput, calls=%fused_computation.13 | convolution fusion | flops 3222208512 | bytes 8388608 | tf_op jit(solution)/shard_map/pmac,cd->pmad/dot_general | solution.py:34
  170.7 8.4 %fusion.54 = f32[2,8,256,256]{3,2,1,0:T(8,128)S(1)} fusion(f32[2,8,256,256]{3,2,1,0:T(8,128)S(1)} %fusion.17, f32[2,256,256]{2,1,0:T(8,128)S(1)} %get-tuple-element.73, f32[8,256,256]{2,1,0:T(8,128)S(1)} %copy-done, f32[2,256,256]{2,1,0:T(8,128)S(1)} %get-tuple-element.72, f32[8,256,256]{2,1,0:T(8,128)S(1)} %get-tuple-element.70), kind=kOutput, calls=%fused_computation.55 | convolution fusion | flops 3226402816 | bytes 13631488 | tf_op jit(solution)/shard_map/ab,pmbc->pmac/dot_general | solution.py:25
  179.1 8.4 %fusion.34 = f32[2,8,256,256]{3,2,1,0:T(8,128)S(1)} fusion(f32[2,8,256,256]{3,2,1,0:T(8,128)S(1)} %fusion.10, f32[2,8,256,256]{3,2,1,0:T(8,128)S(1)} %fusion.54), kind=kOutput, calls=%fused_computation.42 | convolution fusion | flops 3223257088 | bytes 12582912 | tf_op jit(solution)/shard_map/pmac,cd->pmad/dot_general | solution.py:31
  187.6 9.1 %add_reduce_fusion.2 = (f32[2,256,256]{2,1,0:T(8,128)S(1)}, f32[2,8,256,256]{3,2,1,0:T(8,128)S(1)}) fusion(f32[2,8,256,256]{3,2,1,0:T(8,128)S(1)} %fusion.34, f32[2,8,256,256]{3,2,1,0:T(8,128)S(1)} %fusion.8, f32[2,8,256,256]{3,2,1,0:T(8,128)S(1)} %fusion.54), kind=kOutput, calls=%fused_computation.25 | convolution fusion | flops 3227320320 | bytes 17301504 | tf_op jit(solution)/shard_map/pmac,cd->pmad/dot_general | solution.py:34
  196.9 7.6 %fusion.22 = f32[2,8,256,256]{3,2,1,0:T(8,128)S(1)} fusion(f32[2,8,256,256]{3,2,1,0:T(8,128)S(1)} %get-tuple-element.83, f32[2,256,256]{2,1,0:T(8,128)S(1)} %subtract_multiply_fusion), kind=kOutput, calls=%fused_computation.34 | convolution fusion | flops 3223322624 | bytes 8912896 | tf_op jit(solution)/shard_map/ab,pmbc->pmac/dot_general | solution.py:25
  204.6 8.4 %fusion.20 = f32[2,8,256,256]{3,2,1,0:T(8,128)S(1)} fusion(f32[2,8,256,256]{3,2,1,0:T(8,128)S(1)} %get-tuple-element.83, f32[2,256,256]{2,1,0:T(8,128)S(1)} %subtract_multiply_fusion), kind=kOutput, calls=%fused_computation.32 | convolution fusion | flops 3223257088 | bytes 8912896 | tf_op jit(solution)/shard_map/ab,pmbc->pmac/dot_general | solution.py:28
  212.9 8.4 %fusion.31 = f32[2,8,256,256]{3,2,1,0:T(8,128)S(1)} fusion(f32[2,8,256,256]{3,2,1,0:T(8,128)S(1)} %fusion.20, f32[2,8,256,256]{3,2,1,0:T(8,128)S(1)} %fusion.34, f32[2,256,256]{2,1,0:T(8,128)S(1)} %subtract_multiply_fusion), kind=kOutput, calls=%fused_computation.41 | convolution fusion | flops 3224371200 | bytes 13107200 | tf_op jit(solution)/shard_map/ab,pmbc->pmac/dot_general | solution.py:28
  221.3 8.2 %fusion.2 = f32[2,8,256,256]{3,2,1,0:T(8,128)S(1)} fusion(f32[2,8,256,256]{3,2,1,0:T(8,128)S(1)} %fusion.31), kind=kOutput, calls=%fused_computation.7 | convolution fusion | flops 3222274048 | bytes 8388608 | tf_op jit(solution)/shard_map/pmac,cd->pmad/dot_general | solution.py:31
  229.5 8.3 %fusion = f32[2,8,256,256]{3,2,1,0:T(8,128)S(1)} fusion(f32[2,8,256,256]{3,2,1,0:T(8,128)S(1)} %fusion.31), kind=kOutput, calls=%fused_computation.5 | convolution fusion | flops 3222208512 | bytes 8388608 | tf_op jit(solution)/shard_map/pmac,cd->pmad/dot_general | solution.py:34
  237.8 8.5 %fusion.28 = f32[2,8,256,256]{3,2,1,0:T(8,128)S(1)} fusion(f32[2,8,256,256]{3,2,1,0:T(8,128)S(1)} %fusion.22, f32[2,8,256,256]{3,2,1,0:T(8,128)S(1)} %fusion.34, f32[2,256,256]{2,1,0:T(8,128)S(1)} %subtract_multiply_fusion), kind=kOutput, calls=%fused_computation.40 | convolution fusion | flops 3224305664 | bytes 13107200 | tf_op jit(solution)/shard_map/ab,pmbc->pmac/dot_general | solution.py:25
  246.3 8.3 %fusion.40 = f32[2,8,256,256]{3,2,1,0:T(8,128)S(1)} fusion(f32[2,8,256,256]{3,2,1,0:T(8,128)S(1)} %fusion.2, f32[2,8,256,256]{3,2,1,0:T(8,128)S(1)} %fusion.28), kind=kOutput, calls=%fused_computation.44 | convolution fusion | flops 3223257088 | bytes 12582912 | tf_op jit(solution)/shard_map/pmac,cd->pmad/dot_general | solution.py:31
  254.7 13.2 %add_reduce_fusion = (f32[8,256,256]{2,1,0:T(8,128)}, f32[8,256,256]{2,1,0:T(8,128)}, f32[2,256,256]{2,1,0:T(8,128)S(1)}, f32[2,256,256]{2,1,0:T(8,128)S(1)}) fusion(f32[2,8,256,256]{3,2,1,0:T(8,128)S(1)} %fusion.40, f32[2,256,256]{2,1,0:T(8,128)S(1)} %get-tuple-element.73, f32[2,256,256]{2,1,0:T(8,128)S(1)} %get-tuple-element.72, ...), kind=kOutput, calls=%fused_computation.22 | convolution fusion | flops 3238789120 | bytes 23068672 | tf_op jit(solution)/shard_map/pmac,cd->pmad/dot_general | solution.py:34
  268.0 4.3 broadcast_in_dim.6
  272.3 6.7 %dynamic_update_slice.6 = f32[2,1024,1024]{2,1,0:T(8,128)} dynamic-update-slice(f32[2,1024,1024]{2,1,0:T(8,128)} %broadcast_in_dim.6, f32[2,256,256]{2,1,0:T(8,128)S(1)} %pad_maximum_fusion.2, s32[]{:T(128)} %constant.90.clone.1, s32[]{:T(128)S(6)} %select_n.60, s32[]{:T(128)S(6)} %select_n.61) | dynamic-update-slice | bytes 1048580 | tf_op jit(solution)/shard_map/dynamic_update_slice | solution.py:81
  280.4 6.8 %dynamic_update_slice.7 = f32[2,1024,1024]{2,1,0:T(8,128)} dynamic-update-slice(f32[2,1024,1024]{2,1,0:T(8,128)} %dynamic_update_slice.6, f32[2,256,256]{2,1,0:T(8,128)S(1)} %maximum_add_fusion, s32[]{:T(128)} %constant.90.clone.1, s32[]{:T(128)S(6)} %select_n.62, s32[]{:T(128)S(6)} %select_n.63) | dynamic-update-slice | bytes 1048580 | tf_op jit(solution)/shard_map/dynamic_update_slice | solution.py:81
  289.8 3.9 collective-permute-start.2
  293.7 70.7 %collective-permute-done.2 = f32[2,512,1024]{2,1,0:T(8,128)S(1)} collective-permute-done((f32[2,512,1024]{2,1,0:T(8,128)S(1)}, f32[2,512,1024]{2,1,0:T(8,128)S(1)}, u32[]{:S(2)}, u32[]{:S(2)}) %collective-permute-start.2) | collective-permute-done | bytes 4194336 | tf_op jit(solution)/shard_map/ppermute | solution.py:12
  369.3 42.5 %collective-permute-start.3 = (f32[2,512,512]{2,1,0:T(8,128)}, f32[2,512,512]{2,1,0:T(8,128)S(1)}, u32[]{:S(2)}, u32[]{:S(2)}) collective-permute-start(f32[2,512,512]{2,1,0:T(8,128)} %slice.124), channel_id=1, source_target_pairs={{0,1},{1,2},{2,3},{3,4},{4,5},{5,6},{6,7},{7,8},{8,9},{9,10},{10,1... | collective-permute-start | bytes 6291464 | tf_op jit(solution)/shard_map/ppermute | solution.py:12
  414.2 23.7 %collective-permute-done.3 = f32[2,512,512]{2,1,0:T(8,128)S(1)} collective-permute-done((f32[2,512,512]{2,1,0:T(8,128)}, f32[2,512,512]{2,1,0:T(8,128)S(1)}, u32[]{:S(2)}, u32[]{:S(2)}) %collective-permute-start.3) | collective-permute-done | bytes 2097184 | tf_op jit(solution)/shard_map/ppermute | solution.py:12
  437.9 3.4 slice_add_fusion.1
  441.4 133.0 %all-reduce.2.cloned.1.call-done = f32[2,8,256,256]{3,2,1,0:T(8,128)} async-done(((f32[2,8,256,256]{3,2,1,0:T(8,128)}), f32[2,8,256,256]{3,2,1,0:T(8,128)}) %all-reduce.2.cloned.1.call-update) | async-done | bytes 4194320 | tf_op jit(solution)/shard_map/psum | solution.py:72
  574.4 4.6 copy.55
  (47 shorter events, 27.2 us)
Async XLA Ops:
  7.2 31.7 %copy-start.6 = (s32[2]{0:T(128)S(1)}, s32[2]{0:T(128)}, u32[]{:S(2)}) copy-start(s32[2]{0:T(128)} %param.17) | copy-start | bytes 28
  7.2 33.5 %copy-start.7 = (s32[2]{0:T(128)S(1)}, s32[2]{0:T(128)}, u32[]{:S(2)}) copy-start(s32[2]{0:T(128)} %param.18) | copy-start | bytes 28
  7.2 38.1 %copy-start.8 = (s32[2]{0:T(128)S(1)}, s32[2]{0:T(128)}, u32[]{:S(2)}) copy-start(s32[2]{0:T(128)} %param.19) | copy-start | bytes 28
  7.2 567.2 %all-reduce.2.cloned.1.call-start = ((), (), s32[]{:S(2)}) async-start(), calls=%async_computation | async-start | bytes 8388608 | tf_op jit(solution)/shard_map/psum | solution.py:72
  7.2 28.8 %collective-permute-start = (f32[2,512,512]{2,1,0:T(8,128)}, f32[2,512,512]{2,1,0:T(8,128)S(1)}, u32[]{:S(2)}, u32[]{:S(2)}) collective-permute-start(f32[2,512,512]{2,1,0:T(8,128)} %param.14), channel_id=1, source_target_pairs={{1,0},{2,1},{3,2},{4,3},{5,4},{6,5},{7,6},{8,7},{9,8},{10,9},{11,1... | collective-permute-start | bytes 6291464 | tf_op jit(solution)/shard_map/ppermute | solution.py:12
  37.5 73.8 %collective-permute-start.1 = (f32[2,512,1024]{2,1,0:T(8,128)}, f32[2,512,1024]{2,1,0:T(8,128)}, u32[]{:S(2)}, u32[]{:S(2)}) collective-permute-start(f32[2,512,1024]{2,1,0:T(8,128)} %constant_dynamic-update-slice_fusion), channel_id=1, source_target_pairs={{16,0},{32,16},{48,32},{64,48},{80,64},{96,80},{112,96},{17,1},{33... | collective-permute-start | bytes 12582920 | tf_op jit(solution)/shard_map/ppermute | solution.py:12
  126.9 1.6 copy-start
  187.6 9.1 %copy-start.5 = (f32[2,256,256]{2,1,0:T(8,128)S(1)}, f32[2,256,256]{2,1,0:T(8,128)}, u32[]{:S(2)}) copy-start(f32[2,256,256]{2,1,0:T(8,128)} %param.16) | copy-start | bytes 1572868
  287.1 77.2 %copy-start.1 = (f32[2,1024,1024]{2,1,0:T(8,128)S(1)}, f32[2,1024,1024]{2,1,0:T(8,128)}, u32[]{:S(2)}) copy-start(f32[2,1024,1024]{2,1,0:T(8,128)} %dynamic_update_slice.7) | copy-start | bytes 25165828
  289.8 74.6 %collective-permute-start.2 = (f32[2,512,1024]{2,1,0:T(8,128)S(1)}, f32[2,512,1024]{2,1,0:T(8,128)S(1)}, u32[]{:S(2)}, u32[]{:S(2)}) collective-permute-start(f32[2,512,1024]{2,1,0:T(8,128)S(1)} %slice.122), channel_id=1, source_target_pairs={{0,16},{16,32},{32,48},{48,64},{64,80},{80,96},{96,112},{1,17},{17... | collective-permute-start | bytes 12582920 | tf_op jit(solution)/shard_map/ppermute | solution.py:12
  365.7 2.0 copy-start.2
  367.7 44.0 %copy-start.3 = (f32[8,256,256]{2,1,0:T(8,128)S(1)}, f32[8,256,256]{2,1,0:T(8,128)}, u32[]{:S(2)}) copy-start(f32[8,256,256]{2,1,0:T(8,128)} %get-tuple-element.56) | copy-start | bytes 6291460
  367.8 44.0 %copy-start.4 = (f32[8,256,256]{2,1,0:T(8,128)S(1)}, f32[8,256,256]{2,1,0:T(8,128)}, u32[]{:S(2)}) copy-start(f32[8,256,256]{2,1,0:T(8,128)} %get-tuple-element.57) | copy-start | bytes 6291460
  369.3 68.7 %collective-permute-start.3 = (f32[2,512,512]{2,1,0:T(8,128)}, f32[2,512,512]{2,1,0:T(8,128)S(1)}, u32[]{:S(2)}, u32[]{:S(2)}) collective-permute-start(f32[2,512,512]{2,1,0:T(8,128)} %slice.124), channel_id=1, source_target_pairs={{0,1},{1,2},{2,3},{3,4},{4,5},{5,6},{6,7},{7,8},{8,9},{9,10},{10,1... | collective-permute-start | bytes 6291464 | tf_op jit(solution)/shard_map/ppermute | solution.py:12
Sparse Core Ops, SparseCore 0:
  414.3 160.0 all-reduce.1
where the time goes:
time: 589 us; the launch traced here: 586 us
  waiting for transfers between devices  309 us (52%)
  matrix products  139 us (24%)
  starting transfers between devices  51 us (9%)
  local copies, waits for them, and re-layouts  46.7 us (8%)
  between operations  22.2 us (4%)
  other arithmetic  17.2 us (3%)
    ppermute x4, waiting for transfers between devices, passed_along(): return lax.ppermute(array, axis, pairs)  176 us
    psum x1, waiting for transfers between devices, shards(): probe_grad = lax.psum(partial_probe, ('row', 'col'))  133 us
    ppermute x4, starting transfers between devices, passed_along(): return lax.ppermute(array, axis, pairs)  51 us
    dot_general x2, matrix products, transform(): jnp.einsum('pmac,cd->pmad', left_re, sine, precision=best)  22.3 us
    dot_general x2, matrix products, transform(): jnp.einsum('ab,pmbc->pmac', cosine, field_re, precision=best)  16.9 us
    dot_general x2, matrix products, transform(): jnp.einsum('ab,pmbc->pmac', cosine, field_im, precision=best)  16.9 us
    dot_general x2, matrix products, transform(): jnp.einsum('pmac,cd->pmad', left_re, cosine, precision=best)  16.8 us
    dot_general x2, matrix products, transform(): jnp.einsum('ab,pmbc->pmac', sine, field_re, precision=best)  16.8 us
  transfers between devices with their start and end apart: 5, of which 5 were waited for; matrix products, arithmetic and copies ran while one was open for 2% of the time, Pallas kernels for 0%

commit v1 on v0

v1 whole, which is shorter than its diff:
```python
import functools
import jax
import jax.numpy as jnp
import numpy as np
from jax import lax
from jax.experimental import pallas as pl
from jax.experimental.pallas import tpu as pltpu
from jax.sharding import PartitionSpec as P

BF = jnp.bfloat16
F32 = jnp.float32
W, MODES, TILE, EXT, HALF = 256, 8, 512, 768, 128


def split_np(m):
    hi = m.astype(np.float32).astype(jnp.bfloat16)
    lo = (m - hi.astype(np.float64)).astype(np.float32).astype(jnp.bfloat16)
    return hi, lo


def tables():
    n = np.arange(HALF)
    out = []
    for odd in (0, 1):
        k = 2 * np.arange(HALF) + odd
        phase = 2.0 * np.pi * ((k[:, None] * n[None, :]) % W) / W
        c, s = np.cos(phase) / 16.0, np.sin(phase) / 16.0
        m = np.block([[c, s], [-s, c]])
        for t in (m, m.T):
            out.extend(split_np(t))
    return np.stack(out)


def column_order():
    q = np.zeros((W, W), np.float32)
    for j in range(HALF):
        q[2 * j, j] = 1.0
        q[2 * j + 1, HALF + j] = 1.0
    return np.stack([q, q.T]).astype(jnp.bfloat16)


def parts(x):
    hi = x.astype(BF)
    lo = (x - hi.astype(F32)).astype(BF)
    return hi, lo


def dot(a, b):
    return jnp.dot(a, b, preferred_element_type=F32)


def left(tab, i, data):
    hi, lo = parts(data)
    return dot(tab[i], hi) + dot(tab[i + 1], hi) + dot(tab[i], lo)


def right(data, tab, i):
    hi, lo = parts(data)
    return dot(hi, tab[i]) + dot(hi, tab[i + 1]) + dot(lo, tab[i])


ME, MET, MO, MOT = 0, 2, 4, 6


def transform(re, im, tab):
    even = jnp.concatenate([re[:HALF] + re[HALF:], im[:HALF] + im[HALF:]], 0)
    odd = jnp.concatenate([re[:HALF] - re[HALF:], im[:HALF] - im[HALF:]], 0)
    ye = left(tab, ME, even)
    yo = left(tab, MO, odd)
    a = jnp.concatenate([
        jnp.concatenate([y[:HALF, :HALF] + y[:HALF, HALF:], y[HALF:, :HALF] + y[HALF:, HALF:]], 1) for y in (ye, yo)], 0)
    b = jnp.concatenate([
        jnp.concatenate([y[:HALF, :HALF] - y[:HALF, HALF:], y[HALF:, :HALF] - y[HALF:, HALF:]], 1) for y in (ye, yo)], 0)
    return right(a, tab, MET), right(b, tab, MOT)


def inverse(fe, fo, tab):
    ge = right(fe, tab, ME)
    go = right(fo, tab, MO)
    p, q = ge + go, ge - go
    even = jnp.concatenate([
        jnp.concatenate([p[:HALF, :HALF], q[:HALF, :HALF]], 1),
        jnp.concatenate([p[:HALF, HALF:], q[:HALF, HALF:]], 1)], 0)
    odd = jnp.concatenate([
        jnp.concatenate([p[HALF:, :HALF], q[HALF:, :HALF]], 1),
        jnp.concatenate([p[HALF:, HALF:], q[HALF:, HALF:]], 1)], 0)
    a = left(tab, MET, even)
    b = left(tab, MOT, odd)
    s, d = a + b, a - b
    return jnp.concatenate([s[:HALF], d[:HALF]], 0), jnp.concatenate([s[HALF:], d[HALF:]], 0)


def lanes_left(blocks, shift):
    lane = lax.broadcasted_iota(jnp.int32, blocks[0].shape, 1)
    turned = [pltpu.roll(x, lax.rem(HALF - shift, HALF), 1) for x in blocks]
    keep = lane < HALF - shift
    return [jnp.where(keep, turned[j], turned[j + 1]) for j in range(len(blocks) - 1)]


def lanes_right(blocks, shift):
    lane = lax.broadcasted_iota(jnp.int32, blocks[0].shape, 1)
    turned = [pltpu.roll(x, shift, 1) for x in blocks]
    turned = [jnp.zeros_like(blocks[0])] + turned + [jnp.zeros_like(blocks[0])]
    keep = lane >= shift
    return [jnp.where(keep, turned[j + 1], turned[j]) for j in range(len(blocks) + 1)]


def compute_kernel(top_ref, col_ref, live_ref, obj_hbm, low_hbm, right_hbm, probe_ref, int_ref, tab, perm_ref,
                   gmain_ref, gright_ref, pg_ref, ext, grad, patch, spec, contrib, amp, sems):
    copies = [
        pltpu.make_async_copy(obj_hbm, ext.at[:, pl.ds(0, TILE), pl.ds(0, TILE)], sems.at[0]),
        pltpu.make_async_copy(low_hbm, ext.at[:, pl.ds(TILE, W), pl.ds(0, TILE)], sems.at[1]),
        pltpu.make_async_copy(right_hbm, ext.at[:, :, pl.ds(TILE, W)], sems.at[2]),
    ]
    for c in copies:
        c.start()
    grad[...] = jnp.zeros_like(grad)
    contrib[...] = jnp.zeros_like(contrib)
    amp[...] = jnp.zeros_like(amp)
    for c in copies:
        c.wait()
    for k in range(2):
        t = top_ref[k]
        l = col_ref[k]
        base = pl.multiple_of(l // HALF * HALF, HALF)
        start = pl.multiple_of(t // 8 * 8, 8)
        for c in range(2):
            rows = ext[c, pl.ds(start, W + 8), pl.ds(base, 3 * HALF)]
            rows = pltpu.roll(rows, W + 8 - (t - start), 0)[:W]
            got = lanes_left([rows[:, j * HALF:(j + 1) * HALF] for j in range(3)], l - base)
            patch[k, c] = jnp.concatenate(got, 1)

    def forward(m, carry):
        pr, pi = probe_ref[0, m], probe_ref[1, m]
        for k in range(2):
            o_r, o_i = patch[k, 0], patch[k, 1]
            fe, fo = transform(pr * o_r - pi * o_i, pr * o_i + pi * o_r, tab)
            spec[k, m, 0] = fe
            spec[k, m, 1] = fo
            fe2, fo2 = fe * fe, fo * fo
            amp[k] += jnp.concatenate([fe2[:, :HALF] + fe2[:, HALF:], fo2[:, :HALF] + fo2[:, HALF:]], 1)
        return carry

    lax.fori_loop(0, MODES, forward, 0)

    for k in range(2):
        hi, lo = parts(jnp.sqrt(int_ref[k]))
        hi, lo = dot(perm_ref[1], hi).astype(BF), dot(perm_ref[1], lo).astype(BF)
        root = dot(hi, perm_ref[0]) + dot(lo, perm_ref[0])
        alive = live_ref[k].astype(F32)
        amp[k] = (1.0 - root / jnp.sqrt(amp[k] + 0.25)) * alive

    def backward(m, carry):
        pr, pi = probe_ref[0, m], probe_ref[1, m]
        gr = gi = None
        for k in range(2):
            o_r, o_i = patch[k, 0], patch[k, 1]
            f = amp[k]
            fe, fo = f[:, :HALF], f[:, HALF:]
            chi_r, chi_i = inverse(spec[k, m, 0] * jnp.concatenate([fe, fe], 1), spec[k, m, 1] * jnp.concatenate([fo, fo], 1), tab)
            contrib[k, 0] += pr * chi_r + pi * chi_i
            contrib[k, 1] += pr * chi_i - pi * chi_r
            qr = o_r * chi_r + o_i * chi_i
            qi = o_r * chi_i - o_i * chi_r
            gr = qr if gr is None else gr + qr
            gi = qi if gi is None else gi + qi
        pg_ref[0, m] = gr
        pg_ref[1, m] = gi
        return carry

    lax.fori_loop(0, MODES, backward, 0)

    for k in range(2):
        t = top_ref[k]
        l = col_ref[k]
        base = pl.multiple_of(l // HALF * HALF, HALF)
        start = pl.multiple_of(t // 8 * 8, 8)
        for c in range(2):
            g = contrib[k, c]
            wide = jnp.concatenate(lanes_right([g[:, :HALF], g[:, HALF:]], l - base), 1)
            wide = pltpu.roll(jnp.concatenate([wide, jnp.zeros((8, 3 * HALF), F32)], 0), t - start, 0)
            grad[c, pl.ds(start, W + 8), pl.ds(base, 3 * HALF)] += wide
    out = [
        pltpu.make_async_copy(grad.at[:, :, pl.ds(0, TILE)], gmain_ref, sems.at[0]),
        pltpu.make_async_copy(grad.at[:, :, pl.ds(TILE, W)], gright_ref, sems.at[1]),
    ]
    for c in out:
        c.start()
    for c in out:
        c.wait()


def compute(top, col, live, obj, low, rgt, probe, intensity):
    tab = jnp.asarray(tables())
    perm = jnp.asarray(column_order())
    smem = pl.BlockSpec(memory_space=pltpu.SMEM)
    vmem = pl.BlockSpec(memory_space=pltpu.VMEM)
    hbm = pl.BlockSpec(memory_space=pl.ANY)
    return pl.pallas_call(
        compute_kernel,
        out_shape=(
            jax.ShapeDtypeStruct((2, EXT, TILE), F32),
            jax.ShapeDtypeStruct((2, EXT, W), F32),
            jax.ShapeDtypeStruct((2, MODES, W, W), F32),
        ),
        in_specs=[smem, smem, smem, hbm, hbm, hbm, vmem, vmem, vmem, vmem],
        out_specs=(hbm, hbm, vmem),
        scratch_shapes=[
            pltpu.VMEM((2, EXT, EXT), F32),
            pltpu.VMEM((2, EXT, EXT), F32),
            pltpu.VMEM((2, 2, W, W), F32),
            pltpu.VMEM((2, MODES, 2, W, W), F32),
            pltpu.VMEM((2, 2, W, W), F32),
            pltpu.VMEM((2, W, W), F32),
            pltpu.SemaphoreType.DMA((3,)),
        ],
        compiler_params=pltpu.CompilerParams(vmem_limit_bytes=60 * 1024 * 1024),
        name="ptycho",
    )(top, col, live, obj, low, rgt, probe, intensity, tab, perm)


def along(array, axis, by):
    devices = lax.axis_size(axis)
    pairs = [(i, i + by) for i in range(devices) if 0 <= i + by < devices]
    return lax.ppermute(array, axis, pairs)


def shards(object_field, probe, intensity, row_offset, col_offset, live):
    low = along(object_field[:, :W, :], "row", -1)
    rgt = along(jnp.concatenate([object_field[:, :, :W], low[:, :, :W]], axis=1), "col", -1)
    gmain, gright, partial_probe = compute(row_offset, col_offset, live, object_field, low, rgt, probe, intensity)
    probe_grad = lax.psum(partial_probe, ("row", "col"))
    back = along(gright, "col", 1)
    gmain = gmain.at[:, :, :W].add(back)
    down = along(gmain[:, TILE:, :], "row", 1)
    object_grad = gmain[:, :TILE, :].at[:, :W, :].add(down)
    return (object_grad, probe_grad)


def solution(mesh):
    in_specs = (
        P(None, "row", "col"),
        P(),
        P(("row", "col"), None, None),
        P(("row", "col")),
        P(("row", "col")),
        P(("row", "col")),
    )
    out_specs = (P(None, "row", "col"), P())
    return jax.shard_map(shards, mesh=mesh, in_specs=in_specs, out_specs=out_specs, check_vma=False)
```

time: 589 us -> 300 us (0.51)
  matrix products: 139 us -> 0 us
  waiting for transfers between devices: 309 us -> 228 us
  starting transfers between devices: 51 us -> 10.1 us
  local copies, waits for them, and re-layouts: 46.7 us -> 8.73 us
  Pallas kernels: 0 us -> 35.3 us
  other arithmetic: 17.2 us -> 3.09 us
  between operations: 22.2 us -> 14.1 us
    dot_general x16 -> x0, matrix products: 139 us -> none  [the longest x2 22.3 us: transform(): jnp.einsum('pmac,cd->pmad', left_re, sine, precision=best)]
    ppermute x4, waiting for transfers between devices: 176 us -> 74.3 us  [along(): return lax.ppermute(array, axis, pairs)]
    ppermute x4, starting transfers between devices: 51 us -> 10 us  [along(): return lax.ppermute(array, axis, pairs)]
    pallas_call x0 -> x1, Pallas kernels: none -> 35.3 us  [compute(): pl.pallas_call(compute_kernel, out_shape=(jax.ShapeDtypeStruct((2, EXT, T...]
    psum x1, waiting for transfers between devices: 133 us -> 154 us  [shards(): probe_grad = lax.psum(partial_probe, ('row', 'col'))]
    dynamic_update_slice x2 -> x0, local copies, waits for them, and re-layouts: 13.5 us -> none  [shards(): lax.dynamic_update_slice(grad_ext, current + contrib, (anchor, top, left))]
    concatenate x2 -> x1, other arithmetic: 8.43 us -> 0.1 us  [shards(): jnp.concatenate([object_field[:, :, :W], low[:, :, :W]], axis=1)]
    gather x6 -> x0, local copies, waits for them, and re-layouts: 6.71 us -> none
where the time goes in v1:
time: 300 us
  waiting for transfers between devices  228 us (76%)
  Pallas kernels  35.3 us (12%)
  between operations  14.1 us (5%)
  starting transfers between devices  10.1 us (3%)
  local copies, waits for them, and re-layouts  8.73 us (3%)
  other arithmetic  3.09 us (1%)
    psum x1, waiting for transfers between devices, shards(): probe_grad = lax.psum(partial_probe, ('row', 'col'))  154 us
    ppermute x4, waiting for transfers between devices, along(): return lax.ppermute(array, axis, pairs)  74.3 us
    pallas_call x1, Pallas kernels, compute(): pl.pallas_call(compute_kernel, out_shape=(jax.ShapeDtypeStruct((2, EXT, T...  35.3 us
    ppermute x4, starting transfers between devices, along(): return lax.ppermute(array, axis, pairs)  10 us
  transfers between devices with their start and end apart: 5, of which 5 were waited for; matrix products, arithmetic and copies ran while one was open for 2% of the time, Pallas kernels for 0%

profile of v1, /device:TPU:1, one launch (start us, length us, event | category | flops | bytes accessed | tf_op | source)
XLA Modules:
  0.0 299.5 jit_solution(6253099155305020788)
XLA Ops:
  7.2 0.0 slice-start
  7.2 0.0 all-reduce.2.cloned.1.call-start
  7.2 1.4 slice.64
  8.6 1.3 collective-permute-start
  9.9 25.2 %collective-permute-done.low_hbm = f32[2,256,512]{2,1,0:T(8,128)S(1)} collective-permute-done((f32[2,256,512]{2,1,0:T(8,128)S(1)}, f32[2,256,512]{2,1,0:T(8,128)S(1)}, u32[]{:S(2)}, u32[]{:S(2)}) %collective-permute-start) | collective-permute-done | bytes 1048608 | tf_op jit(solution)/shard_map/ppermute | solution.py:225
  35.1 0.0 copy-start.1
  35.2 0.0 slice-done
  35.2 0.1 pad_maximum_fusion
  35.3 3.5 %collective-permute-start.1 = (f32[2,768,256]{2,1,0:T(8,128)S(1)}, f32[2,768,256]{2,1,0:T(8,128)S(1)}, u32[]{:S(2)}, u32[]{:S(2)}) collective-permute-start(f32[2,768,256]{2,1,0:T(8,128)S(1)} %pad_maximum_fusion), channel_id=1, source_target_pairs={{1,0},{2,1},{3,2},{4,3},{5,4},{6,5},{7,6},{8,7},{9,8},{10,9},{11,1... | collective-permute-start | bytes 4718600 | tf_op jit(solution)/shard_map/ppermute | solution.py:225
  38.8 19.3 %collective-permute-done.1.right_hbm = f32[2,768,256]{2,1,0:T(8,128)S(1)} collective-permute-done((f32[2,768,256]{2,1,0:T(8,128)S(1)}, f32[2,768,256]{2,1,0:T(8,128)S(1)}, u32[]{:S(2)}, u32[]{:S(2)}) %collective-permute-start.1) | collective-permute-done | bytes 1572896 | tf_op jit(solution)/shard_map/ppermute | solution.py:225
  58.1 0.0 copy-done.1
  58.2 0.0 copy-start.2
  58.2 1.1 copy-done.2
  59.3 35.3 %ptycho.1 = (f32[2,768,512]{2,1,0:T(8,128)}, f32[2,768,256]{2,1,0:T(8,128)}, f32[2,8,256,256]{3,2,1,0:T(8,128)}) custom-call(s32[2]{0:T(128)} %top_ref.1, s32[2]{0:T(128)} %col_ref.1, s32[2]{0:T(128)} %live_ref.1, f32[2,512,512]{2,1,0:T(8,128)} %obj_hbm.1, f32[2,256,512]{2,1,0:T(8,128)} %copy-done.1, f32[2,768,256]{2,1,0:T(8,128)} %copy-done.2, ...), custom_call_target="tpu_custom_call" | custom-call | tf_op jit(solution)/shard_map/ptycho/pallas_call | solution.py:199
  94.6 1.9 collective-permute-start.2
  96.6 0.0 copy-start
  96.6 0.0 all-reduce.2.cloned.1.call-update
  96.6 19.6 %collective-permute-done.2 = f32[2,768,256]{2,1,0:T(8,128)} collective-permute-done((f32[2,768,256]{2,1,0:T(8,128)}, f32[2,768,256]{2,1,0:T(8,128)}, u32[]{:S(2)}, u32[]{:S(2)}) %collective-permute-start.2) | collective-permute-done | bytes 1572896 | tf_op jit(solution)/shard_map/ppermute | solution.py:225
  116.2 0.0 copy-done
  116.2 1.8 add_dynamic-update-slice_fusion
  118.0 0.1 slice.74
  118.0 3.3 %collective-permute-start.3 = (f32[2,256,512]{2,1,0:T(8,128)S(1)}, f32[2,256,512]{2,1,0:T(8,128)S(1)}, u32[]{:S(2)}, u32[]{:S(2)}) collective-permute-start(f32[2,256,512]{2,1,0:T(8,128)S(1)} %slice.74), channel_id=1, source_target_pairs={{0,16},{16,32},{32,48},{48,64},{64,80},{80,96},{96,112},{1,17},{17... | collective-permute-start | bytes 3145736 | tf_op jit(solution)/shard_map/ppermute | solution.py:225
  121.4 1.5 slice.72
  122.9 10.2 %collective-permute-done.3 = f32[2,256,512]{2,1,0:T(8,128)S(1)} collective-permute-done((f32[2,256,512]{2,1,0:T(8,128)S(1)}, f32[2,256,512]{2,1,0:T(8,128)S(1)}, u32[]{:S(2)}, u32[]{:S(2)}) %collective-permute-start.3) | collective-permute-done | bytes 1048608 | tf_op jit(solution)/shard_map/ppermute | solution.py:225
  133.0 1.2 fusion
  134.2 153.9 %all-reduce.2.cloned.1.call-done = f32[2,8,256,256]{3,2,1,0:T(8,128)} async-done(((f32[2,8,256,256]{3,2,1,0:T(8,128)}), f32[2,8,256,256]{3,2,1,0:T(8,128)}) %all-reduce.2.cloned.1.call-update) | async-done | bytes 4194320 | tf_op jit(solution)/shard_map/psum | solution.py:232
  288.1 4.6 %copy.13 = f32[2,8,256,256]{3,2,1,0:T(8,128)} copy(f32[2,8,256,256]{3,2,1,0:T(8,128)} %all-reduce.2.cloned.1.call-done) | data formatting | bytes 8388608
  (1 shorter events, 0.0 us)
Async XLA Ops:
  7.2 28.0 %slice-start = ((f32[2,512,512]{2,1,0:T(8,128)}), f32[2,512,256]{2,1,0:T(8,128)S(1)}, s32[]{:S(2)}) async-start(f32[2,512,512]{2,1,0:T(8,128)} %obj_hbm.1), calls=%async_computation.1 | async-start | bytes 2097152 | tf_op jit(solution)/shard_map/slice | solution.py:230
  7.2 280.9 %all-reduce.2.cloned.1.call-start = ((), (), s32[]{:S(2)}) async-start(), calls=%async_computation | async-start | bytes 8388608 | tf_op jit(solution)/shard_map/psum | solution.py:232
  8.6 26.5 %collective-permute-start = (f32[2,256,512]{2,1,0:T(8,128)S(1)}, f32[2,256,512]{2,1,0:T(8,128)S(1)}, u32[]{:S(2)}, u32[]{:S(2)}) collective-permute-start(f32[2,256,512]{2,1,0:T(8,128)S(1)} %slice.64), channel_id=1, source_target_pairs={{16,0},{32,16},{48,32},{64,48},{80,64},{96,80},{112,96},{17,1},{33... | collective-permute-start | bytes 3145736 | tf_op jit(solution)/shard_map/ppermute | solution.py:225
  35.1 23.0 %copy-start.1 = (f32[2,256,512]{2,1,0:T(8,128)}, f32[2,256,512]{2,1,0:T(8,128)S(1)}, u32[]{:S(2)}) copy-start(f32[2,256,512]{2,1,0:T(8,128)S(1)} %collective-permute-done.low_hbm) | copy-start | bytes 3145732
  35.3 22.8 %collective-permute-start.1 = (f32[2,768,256]{2,1,0:T(8,128)S(1)}, f32[2,768,256]{2,1,0:T(8,128)S(1)}, u32[]{:S(2)}, u32[]{:S(2)}) collective-permute-start(f32[2,768,256]{2,1,0:T(8,128)S(1)} %pad_maximum_fusion), channel_id=1, source_target_pairs={{1,0},{2,1},{3,2},{4,3},{5,4},{6,5},{7,6},{8,7},{9,8},{10,9},{11,1... | collective-permute-start | bytes 4718600 | tf_op jit(solution)/shard_map/ppermute | solution.py:225
  58.2 1.1 copy-start.2
  94.6 21.5 %collective-permute-start.2 = (f32[2,768,256]{2,1,0:T(8,128)}, f32[2,768,256]{2,1,0:T(8,128)}, u32[]{:S(2)}, u32[]{:S(2)}) collective-permute-start(f32[2,768,256]{2,1,0:T(8,128)} %get-tuple-element.30), channel_id=1, source_target_pairs={{0,1},{1,2},{2,3},{3,4},{4,5},{5,6},{6,7},{7,8},{8,9},{9,10},{10,1... | collective-permute-start | bytes 4718600 | tf_op jit(solution)/shard_map/ppermute | solution.py:225
  96.6 19.6 %copy-start = (f32[2,768,512]{2,1,0:T(8,128)S(1)}, f32[2,768,512]{2,1,0:T(8,128)}, u32[]{:S(2)}) copy-start(f32[2,768,512]{2,1,0:T(8,128)} %get-tuple-element.29) | copy-start | bytes 9437188
  118.0 15.0 %collective-permute-start.3 = (f32[2,256,512]{2,1,0:T(8,128)S(1)}, f32[2,256,512]{2,1,0:T(8,128)S(1)}, u32[]{:S(2)}, u32[]{:S(2)}) collective-permute-start(f32[2,256,512]{2,1,0:T(8,128)S(1)} %slice.74), channel_id=1, source_target_pairs={{0,16},{16,32},{32,48},{48,64},{64,80},{80,96},{96,112},{1,17},{17... | collective-permute-start | bytes 3145736 | tf_op jit(solution)/shard_map/ppermute | solution.py:225
Sparse Core Ops, SparseCore 0:
  96.7 191.3 all-reduce.1

commit v2 on v1

--- a/solution.py
+++ b/solution.py
@@ -219,22 +219,332 @@
     )(top, col, live, obj, low, rgt, probe, intensity, tab, perm)
 
 
-def along(array, axis, by):
-    devices = lax.axis_size(axis)
-    pairs = [(i, i + by) for i in range(devices) if 0 <= i + by < devices]
-    return lax.ppermute(array, axis, pairs)
+MESH = pl.DeviceIdType.MESH
+N_ROW, N_COL = 8, 16
+
+
+def place():
+    row, col = lax.axis_index("row"), lax.axis_index("col")
+    return row, col
+
+
+def remote(src, dst, send, recv, to):
+    return pltpu.make_async_remote_copy(src_ref=src, dst_ref=dst, send_sem=send, recv_sem=recv, device_id=to, device_id_type=MESH)
+
+
+def count(flags):
+    return sum(f.astype(jnp.int32) for f in flags)
+
+
+def gather_kernel(obj, low, rgt, zero, send, recv, zsem):
+    row, col = place()
+    up, down, lft, rht = row > 0, row < N_ROW - 1, col > 0, col < N_COL - 1
+    barrier = pltpu.get_barrier_semaphore()
+    for ok, dev in ((up, (row - 1, col)), (down, (row + 1, col)), (lft, (row, col - 1)), (rht, (row, col + 1))):
+        @pl.when(ok)
+        def _():
+            pl.semaphore_signal(barrier, inc=1, device_id=dev, device_id_type=MESH)
+    pl.semaphore_wait(barrier, count((up, down, lft, rht)))
+    above, left = (lax.max(row - 1, 0), col), (row, lax.max(col - 1, 0))
+    first = remote(obj.at[:, pl.ds(0, W), pl.ds(0, W)], low.at[:, :, pl.ds(0, W)], send.at[0], recv.at[0], above)
+    second = remote(obj.at[:, pl.ds(0, W), pl.ds(W, W)], low.at[:, :, pl.ds(W, W)], send.at[1], recv.at[1], above)
+    side = remote(obj.at[:, :, pl.ds(0, W)], rgt.at[:, pl.ds(0, TILE), :], send.at[2], recv.at[2], left)
+    corner = remote(low.at[:, :, pl.ds(0, W)], rgt.at[:, pl.ds(TILE, W), :], send.at[3], recv.at[3], left)
+
+    @pl.when(up)
+    def _():
+        first.start()
+        second.start()
+
+    @pl.when(lft)
+    def _():
+        side.start()
+
+    edge = jnp.logical_not(jnp.logical_and(down, rht))
+
+    @pl.when(edge)
+    def _():
+        zero[...] = jnp.zeros_like(zero)
+
+    @pl.when(jnp.logical_not(down))
+    def _():
+        for j in range(2):
+            pltpu.make_async_copy(zero, low.at[:, :, pl.ds(j * W, W)], zsem.at[j]).start()
+        for j in range(2):
+            pltpu.make_async_copy(zero, low.at[:, :, pl.ds(j * W, W)], zsem.at[j]).wait()
+
+    @pl.when(jnp.logical_not(rht))
+    def _():
+        for j in range(3):
+            pltpu.make_async_copy(zero, rgt.at[:, pl.ds(j * W, W), :], zsem.at[j]).start()
+        for j in range(3):
+            pltpu.make_async_copy(zero, rgt.at[:, pl.ds(j * W, W), :], zsem.at[j]).wait()
+
+    @pl.when(down)
+    def _():
+        first.wait_recv()
+
+    @pl.when(lft)
+    def _():
+        corner.start()
+
+    @pl.when(down)
+    def _():
+        second.wait_recv()
+
+    @pl.when(rht)
+    def _():
+        side.wait_recv()
+        corner.wait_recv()
+
+    @pl.when(up)
+    def _():
+        first.wait_send()
+        second.wait_send()
+
+    @pl.when(lft)
+    def _():
+        side.wait_send()
+        corner.wait_send()
+
+
+def gather(obj):
+    hbm = pl.BlockSpec(memory_space=pl.ANY)
+    return pl.pallas_call(
+        gather_kernel,
+        out_shape=(jax.ShapeDtypeStruct((2, W, TILE), F32), jax.ShapeDtypeStruct((2, EXT, W), F32)),
+        in_specs=[hbm],
+        out_specs=(hbm, hbm),
+        scratch_shapes=[
+            pltpu.VMEM((2, W, W), F32),
+            pltpu.SemaphoreType.DMA((4,)),
+            pltpu.SemaphoreType.DMA((4,)),
+            pltpu.SemaphoreType.DMA((3,)),
+        ],
+        compiler_params=pltpu.CompilerParams(collective_id=0, has_side_effects=True),
+        name="halo_in",
+    )(obj)
+
+
+UNITS = (3, 2, 3, 3, 2, 3)
+ROWS = 2 * MODES * W
+STREAMS = 6
+STEPS = 5
+
+
+def partners():
+    row, col = place()
+    z_hi, y = row // 4, row % 4
+    z_lo, x, core = col // 8, col // 2 % 4, col % 2
+    z = z_hi * 2 + z_lo
+
+    def dev(x, y, z, core):
+        return (z // 2 * 4 + y, z % 2 * 8 + x * 2 + core)
+
+    def flip(p):
+        return p + 1 - 2 * (p % 2)
+
+    def mirror(p):
+        return 3 - p
+
+    def gray(p):
+        return (p + 1) // 2 % 2
+
+    bits = [
+        (gray(x), dev(flip(x), y, z, core)),
+        (gray(y), dev(x, flip(y), z, core)),
+        (gray(z), dev(x, y, flip(z), core)),
+        (x // 2, dev(mirror(x), y, z, core)),
+        (y // 2, dev(x, mirror(y), z, core)),
+        (z // 2, dev(x, y, mirror(z), core)),
+    ]
+    return bits, core, dev(x, y, z, 1 - core)
+
+
+def reduce_kernel(part, gmain, gright, total, own, data, first, later, gath, tile, add_c, add_r, add_l, asend, arecv, csend, crecv, lsem, osem, hsend, hrecv, gsem):
+    row, col = place()
+    bits, core, twin = partners()
+    up, down, lft, rht = row > 0, row < N_ROW - 1, col > 0, col < N_COL - 1
+    barrier = pltpu.get_barrier_semaphore()
+    for dev in [twin] + [b[1] for b in bits]:
+        pl.semaphore_signal(barrier, inc=1, device_id=dev, device_id_type=MESH)
+    for ok, dev in ((up, (row - 1, col)), (down, (row + 1, col)), (lft, (row, col - 1)), (rht, (row, col + 1))):
+        @pl.when(ok)
+        def _():
+            pl.semaphore_signal(barrier, inc=1, device_id=dev, device_id_type=MESH)
+    mine = pl.ds(pl.multiple_of(core * HALF, HALF), HALF)
+    other = pl.ds(pl.multiple_of((1 - core) * HALF, HALF), HALF)
+    base = [sum(UNITS[:s]) * 256 for s in range(STREAMS)]
+    size = [u * 256 for u in UNITS]
+    loads = [pltpu.make_async_copy(part.at[pl.ds(base[s], size[s]), mine], data.at[pl.ds(base[s], size[s]), :], lsem.at[s]) for s in range(STREAMS)]
+    for c in loads:
+        c.start()
+    halo_loads = [pltpu.make_async_copy(gmain, tile, gsem.at[0])]
+    for c in halo_loads:
+        c.start()
+    pl.semaphore_wait(barrier, 7 + count((up, down, lft, rht)))
+
+    pair = [remote(part.at[pl.ds(base[s], size[s]), other], first.at[pl.ds(base[s], size[s]), :], asend.at[0, s], arecv.at[0, s], twin) for s in range(STREAMS)]
+    for c in pair:
+        c.start()
+
+    below, right = (lax.min(row + 1, N_ROW - 1), col), (row, lax.min(col + 1, N_COL - 1))
+    h_corner = remote(gright.at[:, pl.ds(TILE, W), :], add_c, hsend.at[0], hrecv.at[0], right)
+    h_low1 = remote(gmain.at[:, pl.ds(TILE, W), pl.ds(W, W)], add_l.at[:, :, pl.ds(W, W)], hsend.at[1], hrecv.at[1], below)
+    h_right = remote(gright.at[:, pl.ds(0, TILE), :], add_r, hsend.at[2], hrecv.at[2], right)
+    h_low0 = remote(tile.at[:, pl.ds(TILE, W), pl.ds(0, W)], add_l.at[:, :, pl.ds(0, W)], hsend.at[3], hrecv.at[3], below)
+
+    @pl.when(rht)
+    def _():
+        h_corner.start()
+        h_right.start()
+
+    @pl.when(down)
+    def _():
+        h_low1.start()
+
+    def start_step(i, s, off):
+        g, to = bits[(s + i) % STREAMS]
+        n = size[s] >> (i + 1)
+        send_off = pl.multiple_of(off + (1 - g) * n, 8)
+        keep = pl.multiple_of(off + g * n, 8)
+        spot = base[s] + size[s] - (size[s] >> i)
+        c = remote(data.at[pl.ds(send_off, n), :], later.at[pl.ds(spot, n), :], asend.at[1 + i, s], arecv.at[1 + i, s], to)
+        c.start()
+        return c, keep, n, spot
+
+    offs = []
+    flights = []
+    for s in range(STREAMS):
+        loads[s].wait()
+        pair[s].wait_recv()
+        sl = pl.ds(base[s], size[s])
+        data[sl, :] += first[sl, :]
+        flights.append(start_step(0, s, base[s]))
+        offs.append([base[s]])
+    halo_loads[0].wait()
+
+    @pl.when(lft)
+    def _():
+        h_corner.wait_recv()
+        tile[:, pl.ds(TILE, W), pl.ds(0, W)] += add_c[...]
+
+    @pl.when(down)
+    def _():
+        h_low0.start()
+
+    sends = list(pair)
+    for i in range(STEPS):
+        for s in range(STREAMS):
+            c, keep, n, spot = flights[s]
+            c.wait_recv()
+            sends.append(c)
+            data[pl.ds(keep, n), :] += later[pl.ds(spot, n), :]
+            offs[s].append(keep)
+            if i + 1 < STEPS:
+                flights[s] = start_step(i + 1, s, keep)
+            else:
+                g, to = bits[(s + STEPS) % STREAMS]
+                spot = base[s] + size[s] - n
+                c = remote(data.at[pl.ds(keep, n), :], later.at[pl.ds(spot, n), :], asend.at[1 + STEPS, s], arecv.at[1 + STEPS, s], to)
+                c.start()
+                flights[s] = (c, keep, n, spot)
+    gather_step = []
+    for s in range(STREAMS):
+        c, keep, n, spot = flights[s]
+        c.wait()
+        gath[pl.ds(keep, n), :] = data[pl.ds(keep, n), :] + later[pl.ds(spot, n), :]
+        to = bits[(s + STEPS - 1) % STREAMS][1]
+        here = gath.at[pl.ds(keep, n), :]
+        d = remote(here, here, csend.at[STEPS - 1, s], crecv.at[STEPS - 1, s], to)
+        d.start()
+        gather_step.append(d)
+    for c in sends:
+        c.wait_send()
+    last = []
+    for i in range(STEPS - 1, -1, -1):
+        for s in range(STREAMS):
+            gather_step[s].wait()
+            if i > 0:
+                here = gath.at[pl.ds(offs[s][i], size[s] >> i), :]
+                to = bits[(s + i - 1) % STREAMS][1]
+                d = remote(here, here, csend.at[i - 1, s], crecv.at[i - 1, s], to)
+                d.start()
+                gather_step[s] = d
+            else:
+                sl = pl.ds(base[s], size[s])
+                d = remote(gath.at[sl, :], total.at[sl, mine], csend.at[STEPS, s], crecv.at[STEPS, s], twin)
+                d.start()
+                e = pltpu.make_async_copy(gath.at[sl, :], total.at[sl, mine], osem.at[s])
+                e.start()
+                last += [d, e]
+
+    @pl.when(lft)
+    def _():
+        h_right.wait_recv()
+        tile[:, pl.ds(0, TILE), pl.ds(0, W)] += add_r[...]
+
+    @pl.when(up)
+    def _():
+        h_low1.wait_recv()
+        h_low0.wait_recv()
+        tile[:, pl.ds(0, W), :] += add_l[...]
+
+    result = pltpu.make_async_copy(tile.at[:, pl.ds(0, TILE), :], own, gsem.at[1])
+    result.start()
+
+    @pl.when(rht)
+    def _():
+        h_corner.wait_send()
+        h_right.wait_send()
+
+    @pl.when(down)
+    def _():
+        h_low1.wait_send()
+        h_low0.wait_send()
+
+    for d in last:
+        d.wait()
+    result.wait()
+
+
+def reduce(part, gmain, gright):
+    hbm = pl.BlockSpec(memory_space=pl.ANY)
+    dma = pltpu.SemaphoreType.DMA
+    return pl.pallas_call(
+        reduce_kernel,
+        out_shape=(jax.ShapeDtypeStruct((ROWS, W), F32), jax.ShapeDtypeStruct((2, TILE, TILE), F32)),
+        in_specs=[hbm] * 3,
+        out_specs=(hbm, hbm),
+        scratch_shapes=[
+            pltpu.VMEM((ROWS, HALF), F32),
+            pltpu.VMEM((ROWS, HALF), F32),
+            pltpu.VMEM((ROWS, HALF), F32),
+            pltpu.VMEM((ROWS, HALF), F32),
+            pltpu.VMEM((2, EXT, TILE), F32),
+            pltpu.VMEM((2, W, W), F32),
+            pltpu.VMEM((2, TILE, W), F32),
+            pltpu.VMEM((2, W, TILE), F32),
+            dma((2 + STEPS, STREAMS)),
+            dma((2 + STEPS, STREAMS)),
+            dma((1 + STEPS, STREAMS)),
+            dma((1 + STEPS, STREAMS)),
+            dma((STREAMS,)),
+            dma((STREAMS,)),
+            dma((4,)),
+            dma((4,)),
+            dma((2,)),
+        ],
+        compiler_params=pltpu.CompilerParams(collective_id=1, has_side_effects=True, vmem_limit_bytes=40 * 1024 * 1024),
+        name="reduce_out",
+    )(part, gmain, gright)
 
 
 def shards(object_field, probe, intensity, row_offset, col_offset, live):
-    low = along(object_field[:, :W, :], "row", -1)
-    rgt = along(jnp.concatenate([object_field[:, :, :W], low[:, :, :W]], axis=1), "col", -1)
+    low, rgt = gather(object_field)
     gmain, gright, partial_probe = compute(row_offset, col_offset, live, object_field, low, rgt, probe, intensity)
-    probe_grad = lax.psum(partial_probe, ("row", "col"))
-    back = along(gright, "col", 1)
-    gmain = gmain.at[:, :, :W].add(back)
-    down = along(gmain[:, TILE:, :], "row", 1)
-    object_grad = gmain[:, :TILE, :].at[:, :W, :].add(down)
-    return (object_grad, probe_grad)
+    total, object_grad = reduce(partial_probe.reshape(ROWS, W), gmain, gright)
+    return (object_grad, total.reshape(2, MODES, W, W))
 
 
 def solution(mesh):

time: 300 us -> 163 us (0.54)
  waiting for transfers between devices: 228 us -> 0 us
  Pallas kernels: 35.3 us -> 156 us
  between operations: 14.1 us -> 0.66 us
  starting transfers between devices: 10.1 us -> 0 us
  other arithmetic: 3.09 us -> 0 us
    psum x1 -> x0, waiting for transfers between devices: 154 us -> none  [shards(): probe_grad = lax.psum(partial_probe, ('row', 'col'))]
    pallas_call x0 -> x2, Pallas kernels: none -> 120 us  [the longest x1 92.9 us: reduce(): pl.pallas_call(reduce_kernel, out_shape=(jax.ShapeDtypeStruct((ROWS, W),...]
    ppermute x4 -> x0, waiting for transfers between devices: 74.3 us -> none  [along(): return lax.ppermute(array, axis, pairs)]
    ppermute x4 -> x0, starting transfers between devices: 10 us -> none  [along(): return lax.ppermute(array, axis, pairs)]
    unnamed x7 -> x6, local copies, waits for them, and re-layouts: 5.75 us -> 6.62 us
  transfers between devices with their start and end apart: 5 -> 0, of which waited for: 5 -> 0; matrix products, arithmetic and copies ran while one was open for 2% -> 0% of each run, Pallas kernels for 0% -> 0%
where the time goes in v2:
time: 163 us
  Pallas kernels  156 us (96%)
  local copies, waits for them, and re-layouts  6.62 us (4%)
    pallas_call x1, Pallas kernels, reduce(): pl.pallas_call(reduce_kernel, out_shape=(jax.ShapeDtypeStruct((ROWS, W),...  92.9 us
    pallas_call x1, Pallas kernels, compute(): pl.pallas_call(compute_kernel, out_shape=(jax.ShapeDtypeStruct((2, EXT, T...  35.3 us
    pallas_call x1, Pallas kernels, gather(): pl.pallas_call(gather_kernel, out_shape=(jax.ShapeDtypeStruct((2, W, TILE...  27.5 us
    unnamed x6, local copies, waits for them, and re-layouts  6.62 us

profile of v2, /device:TPU:1, one launch (start us, length us, event | category | flops | bytes accessed | tf_op | source)
XLA Modules:
  0.0 163.0 jit_solution(17456200348813491902)
XLA Ops:
  0.6 27.5 %halo_in.1 = (f32[2,256,512]{2,1,0:T(8,128)}, f32[2,768,256]{2,1,0:T(8,128)}) custom-call(f32[2,512,512]{2,1,0:T(8,128)} %obj_hbm.1), custom_call_target="tpu_custom_call" | custom-call | tf_op jit(solution)/shard_map/halo_in/pallas_call | solution.py:313
  28.1 35.3 %ptycho.1 = (f32[2,768,512]{2,1,0:T(8,128)}, f32[2,768,256]{2,1,0:T(8,128)}, f32[2,8,256,256]{3,2,1,0:T(8,128)}) custom-call(s32[2]{0:T(128)} %top_ref.1, s32[2]{0:T(128)} %col_ref.1, s32[2]{0:T(128)} %live_ref.1, f32[2,512,512]{2,1,0:T(8,128)} %obj_hbm.1, f32[2,256,512]{2,1,0:T(8,128)} %get-tuple-element.9.low_hbm, ...), custom_call_target="tpu_custom_call" | custom-call | tf_op jit(solution)/shard_map/ptycho/pallas_call | solution.py:199
  63.4 0.0 copy-start
  63.4 1.9 %copy-done = f32[2,768,512]{2,1,0:T(8,128)S(1)} copy-done((f32[2,768,512]{2,1,0:T(8,128)S(1)}, f32[2,768,512]{2,1,0:T(8,128)}, u32[]{:S(2)}) %copy-start) | copy-done | bytes 3145752
  65.3 0.0 copy-start.1
  65.3 1.4 copy-done.1
  66.7 92.9 %reduce_out.1 = (f32[4096,256]{1,0:T(8,128)S(1)}, f32[2,512,512]{2,1,0:T(8,128)S(1)}) custom-call(f32[4096,256]{1,0:T(8,128)} %bitcast.3, f32[2,768,512]{2,1,0:T(8,128)S(1)} %copy-done, f32[2,768,256]{2,1,0:T(8,128)S(1)} %copy-done.1), custom_call_target="tpu_custom_call" | custom-call | tf_op jit(solution)/shard_map/reduce_out/pallas_call | solution.py:514
  159.7 1.3 copy.12
  161.0 2.0 %copy.13 = f32[2,8,256,256]{3,2,1,0:T(8,128)} copy(f32[2,8,256,256]{3,2,1,0:T(8,128)S(1)} %bitcast.2) | data formatting | bytes 8388608
Async XLA Ops:
  63.4 1.9 %copy-start = (f32[2,768,512]{2,1,0:T(8,128)S(1)}, f32[2,768,512]{2,1,0:T(8,128)}, u32[]{:S(2)}) copy-start(f32[2,768,512]{2,1,0:T(8,128)} %get-tuple-element.12.gmain) | copy-start | bytes 9437188
  65.3 1.4 copy-start.1

commit v3 on v1

v3 whole, which is shorter than its diff:
```python
import functools
import jax
import jax.numpy as jnp
import numpy as np
from jax import lax
from jax.experimental import pallas as pl
from jax.experimental.pallas import tpu as pltpu
from jax.sharding import PartitionSpec as P

BF = jnp.bfloat16
F32 = jnp.float32
W, MODES, TILE, EXT, HALF = 256, 8, 512, 768, 128


def split_np(m):
    hi = m.astype(np.float32).astype(jnp.bfloat16)
    lo = (m - hi.astype(np.float64)).astype(np.float32).astype(jnp.bfloat16)
    return hi, lo


def tables():
    n = np.arange(HALF)
    out = []
    for odd in (0, 1):
        k = 2 * np.arange(HALF) + odd
        phase = 2.0 * np.pi * ((k[:, None] * n[None, :]) % W) / W
        c, s = np.cos(phase) / 16.0, np.sin(phase) / 16.0
        m = np.block([[c, s], [-s, c]])
        for t in (m, m.T):
            out.extend(split_np(t))
    return np.stack(out)


def column_order():
    q = np.zeros((W, W), np.float32)
    for j in range(HALF):
        q[2 * j, j] = 1.0
        q[2 * j + 1, HALF + j] = 1.0
    return np.stack([q, q.T]).astype(jnp.bfloat16)


def parts(x):
    hi = x.astype(BF)
    lo = (x - hi.astype(F32)).astype(BF)
    return hi, lo


def dot(a, b):
    return jnp.dot(a, b, preferred_element_type=F32)


def left(tab, i, data):
    hi, lo = parts(data)
    return dot(tab[i], hi) + dot(tab[i + 1], hi) + dot(tab[i], lo)


def right(data, tab, i):
    hi, lo = parts(data)
    return dot(hi, tab[i]) + dot(hi, tab[i + 1]) + dot(lo, tab[i])


ME, MET, MO, MOT = 0, 2, 4, 6


def transform(re, im, tab):
    even = jnp.concatenate([re[:HALF] + re[HALF:], im[:HALF] + im[HALF:]], 0)
    odd = jnp.concatenate([re[:HALF] - re[HALF:], im[:HALF] - im[HALF:]], 0)
    ye = left(tab, ME, even)
    yo = left(tab, MO, odd)
    a = jnp.concatenate([
        jnp.concatenate([y[:HALF, :HALF] + y[:HALF, HALF:], y[HALF:, :HALF] + y[HALF:, HALF:]], 1) for y in (ye, yo)], 0)
    b = jnp.concatenate([
        jnp.concatenate([y[:HALF, :HALF] - y[:HALF, HALF:], y[HALF:, :HALF] - y[HALF:, HALF:]], 1) for y in (ye, yo)], 0)
    return right(a, tab, MET), right(b, tab, MOT)


def inverse(fe, fo, tab):
    ge = right(fe, tab, ME)
    go = right(fo, tab, MO)
    p, q = ge + go, ge - go
    even = jnp.concatenate([
        jnp.concatenate([p[:HALF, :HALF], q[:HALF, :HALF]], 1),
        jnp.concatenate([p[:HALF, HALF:], q[:HALF, HALF:]], 1)], 0)
    odd = jnp.concatenate([
        jnp.concatenate([p[HALF:, :HALF], q[HALF:, :HALF]], 1),
        jnp.concatenate([p[HALF:, HALF:], q[HALF:, HALF:]], 1)], 0)
    a = left(tab, MET, even)
    b = left(tab, MOT, odd)
    s, d = a + b, a - b
    return jnp.concatenate([s[:HALF], d[:HALF]], 0), jnp.concatenate([s[HALF:], d[HALF:]], 0)


def picks(shape, axis, offset):
    a, b = lax.broadcasted_iota(jnp.int32, shape, axis), lax.broadcasted_iota(jnp.int32, shape, 1 - axis)
    return jnp.where(a - b == offset, 1.0, 0.0).astype(BF)


def select_left(sel, x):
    hi, lo = parts(x)
    return dot(sel, hi) + dot(sel, lo)


def select_right(x, sel):
    hi, lo = parts(x)
    return dot(hi, sel) + dot(lo, sel)


MESH = pl.DeviceIdType.MESH
N_ROW, N_COL = 8, 16
ROWS = 2 * W
STAGES = 13
RELAY_IN, RELAY_OUT = 1, -1


def remote(src, dst, send, recv, to):
    return pltpu.make_async_remote_copy(src_ref=src, dst_ref=dst, send_sem=send, recv_sem=recv, device_id=to, device_id_type=MESH)


def count(flags):
    return sum(f.astype(jnp.int32) for f in flags)


def both(a, b):
    return jnp.logical_and(a, b)


def hypercube(row, col):
    z_hi, y = row // 4, row % 4
    z_lo, x, core = col // 8, col // 2 % 4, col % 2
    z = z_hi * 2 + z_lo

    def dev(x, y, z):
        return (z // 2 * 4 + y, z % 2 * 8 + x * 2 + core)

    def flip(p):
        return p + 1 - 2 * (p % 2)

    def gray(p):
        return (p + 1) // 2 % 2

    bits = [
        (gray(z),) + dev(x, y, flip(z)),
        (gray(x),) + dev(flip(x), y, z),
        (z // 2,) + dev(x, y, 3 - z),
        (x // 2,) + dev(3 - x, y, z),
    ]
    return bits, core, (row, col + 1 - 2 * core), y, dev(x, (y + 3) % 4, z), dev(x, (y + 1) % 4, z)


def relay_roles(row, col, source, step):
    odd, z_lo = col % 2 == 1, col // 8
    target = 7 - source
    y = source % 4
    first = (source // 4 * 2 + step) % 4
    second = (source // 4 * 2 + 1 + step) % 4
    relay_row = (first // 2 * 4 + y) * (1 - z_lo) + (second // 2 * 4 + y) * z_lo
    is_relay = both(odd, jnp.logical_or(both(row == first // 2 * 4 + y, z_lo == 1), both(row == second // 2 * 4 + y, z_lo == 0)))
    return both(row == source, odd), both(row == target, odd), is_relay, relay_row


def main_kernel(top_ref, col_ref, live_ref, obj, probe_hbm, int_hbm, tab_hbm, perm_hbm, own, total,
                ext, grad, mid, rows_of, cols_of, rows_to, cols_to, patch, spec, contrib, amp, probe, inten, tab, perm, pgm, first, data, later, gath, ring,
                hold_in, hold_out, add_c, add_r, add_l,
                lsem, asend, arecv, osem, isend, irecv, rsend, rrecv, hsend, hrecv, qsend, qrecv):
    row, col = lax.axis_index("row"), lax.axis_index("col")
    bits, core, twin, y, y_next, y_prev = hypercube(row, col)
    up, down, lft, rht = row > 0, row < N_ROW - 1, col > 0, col < N_COL - 1
    in_src, in_dst, in_relay, in_row = relay_roles(row, col, 4, RELAY_IN)
    out_src, out_dst, out_relay, out_row = relay_roles(row, col, 3, RELAY_OUT)
    swap = col + 8 - 16 * (col // 8)
    yes = row >= 0
    no_down, no_rht = jnp.logical_not(down), jnp.logical_not(rht)
    above, below = (lax.max(row - 1, 0), col), (lax.min(row + 1, N_ROW - 1), col)
    left, right = (row, lax.max(col - 1, 0)), (row, lax.min(col + 1, N_COL - 1))

    barrier = pltpu.get_barrier_semaphore()
    peers = [(up, above), (down, below), (lft, left), (rht, right), (yes, twin), (yes, y_next), (yes, y_prev)] + [(yes, b[1:]) for b in bits]
    peers += [(in_src, (in_row, swap)), (in_dst, (in_row, swap)), (in_relay, (4, swap)), (in_relay, (3, swap))]
    peers += [(out_src, (out_row, swap)), (out_dst, (out_row, swap)), (out_relay, (3, swap)), (out_relay, (4, swap))]
    for ok, dev in peers:
        @pl.when(ok)
        def _():
            pl.semaphore_signal(barrier, inc=1, device_id=dev, device_id_type=MESH)

    loads = [
        pltpu.make_async_copy(obj, ext.at[:, pl.ds(0, TILE), pl.ds(0, TILE)], lsem.at[0]),
        pltpu.make_async_copy(probe_hbm, probe, lsem.at[1]),
        pltpu.make_async_copy(tab_hbm, tab, lsem.at[2]),
        pltpu.make_async_copy(int_hbm, inten, lsem.at[3]),
        pltpu.make_async_copy(perm_hbm, perm, lsem.at[4]),
    ]
    pl.semaphore_wait(barrier, count([p[0] for p in peers]))

    pieces = [(c, j) for j in range(2) for c in range(2)]

    def cut(ref, i, start):
        c, j = pieces[i]
        return ref.at[c, pl.ds(start, W), pl.ds(j * W, W)]

    in_direct = [remote(cut(obj, i, 0), cut(ext, i, TILE), isend.at[i], irecv.at[i], above) for i in range(4)]
    in_hop = [remote(cut(obj, i, 0), cut(hold_in, i, 0), rsend.at[i], rrecv.at[i], (in_row, swap)) for i in range(4)]
    in_on = [remote(cut(hold_in, i, 0), cut(ext, i, TILE), rsend.at[4 + i], irecv.at[i], (3, swap)) for i in range(4)]
    side = remote(obj.at[:, :, pl.ds(0, W)], ext.at[:, pl.ds(0, TILE), pl.ds(TILE, W)], isend.at[4], irecv.at[4], left)
    corner = remote(ext.at[:, pl.ds(TILE, W), pl.ds(0, W)], ext.at[:, pl.ds(TILE, W), pl.ds(TILE, W)], isend.at[5], irecv.at[5], left)
    in_up = both(up, jnp.logical_not(in_src))

    @pl.when(in_src)
    def _():
        for c in in_hop:
            c.start()

    @pl.when(in_up)
    def _():
        for c in in_direct:
            c.start()

    @pl.when(lft)
    def _():
        side.start()

    for c in loads:
        c.start()

    @pl.when(no_down)
    def _():
        ext[:, pl.ds(TILE, W), :] = jnp.zeros((2, W, EXT), F32)

    @pl.when(no_rht)
    def _():
        ext[:, pl.ds(0, TILE), pl.ds(TILE, W)] = jnp.zeros((2, TILE, W), F32)
        ext[:, pl.ds(TILE, W), pl.ds(TILE, W)] = jnp.zeros((2, W, W), F32)

    for k in range(2):
        rows_of[pl.ds(k * W, W), :] = picks((W, EXT), 1, top_ref[k])
        cols_of[k] = picks((EXT, W), 0, col_ref[k])
        rows_to[:, pl.ds(k * W, W)] = picks((EXT, W), 0, top_ref[k])
        cols_to[k] = picks((W, EXT), 1, col_ref[k])
    contrib[...] = jnp.zeros_like(contrib)
    amp[...] = jnp.zeros_like(amp)
    for c in loads:
        c.wait()
    for k in range(2):
        hi, lo = parts(jnp.sqrt(inten[k]))
        hi, lo = dot(perm[1], hi).astype(BF), dot(perm[1], lo).astype(BF)
        inten[k] = dot(hi, perm[0]) + dot(lo, perm[0])

    def rows_own(j):
        for c in range(2):
            cols = pl.ds(j * W, W)
            mid[c, :, cols] = select_left(rows_of[:, :TILE], ext[c, pl.ds(0, TILE), cols])

    rows_own(0)
    rows_own(1)

    @pl.when(in_relay)
    def _():
        for i in range(4):
            in_hop[i].wait_recv()
            in_on[i].start()

    @pl.when(down)
    def _():
        in_direct[0].wait_recv()
        in_direct[1].wait_recv()

    @pl.when(both(down, lft))
    def _():
        corner.start()

    @pl.when(rht)
    def _():
        side.wait_recv()

    rows_own(2)

    @pl.when(down)
    def _():
        in_direct[2].wait_recv()
        in_direct[3].wait_recv()

    @pl.when(both(down, rht))
    def _():
        corner.wait_recv()

    for c in range(2):
        for j in range(3):
            cols = pl.ds(j * W, W)
            mid[c, :, cols] += select_left(rows_of[:, TILE:], ext[c, pl.ds(TILE, W), cols])
        for k in range(2):
            patch[k, c] = select_right(mid[c, pl.ds(k * W, W), :], cols_of[k])

    def forward(m, carry):
        pr, pi = probe[0, m], probe[1, m]
        for k in range(2):
            o_r, o_i = patch[k, 0], patch[k, 1]
            fe, fo = transform(pr * o_r - pi * o_i, pr * o_i + pi * o_r, tab)
            spec[k, m, 0] = fe
            spec[k, m, 1] = fo
            fe2, fo2 = fe * fe, fo * fo
            amp[k] += jnp.concatenate([fe2[:, :HALF] + fe2[:, HALF:], fo2[:, :HALF] + fo2[:, HALF:]], 1)
        return carry

    lax.fori_loop(0, MODES, forward, 0)
    for k in range(2):
        alive = live_ref[k].astype(F32)
        amp[k] = (1.0 - inten[k] / jnp.sqrt(amp[k] + 0.25)) * alive

    mine = pl.ds(pl.multiple_of(core * HALF, HALF), HALF)
    other = pl.ds(pl.multiple_of((1 - core) * HALF, HALF), HALF)

    def backward(m):
        pr, pi = probe[0, m], probe[1, m]
        gr = gi = None
        for k in range(2):
            o_r, o_i = patch[k, 0], patch[k, 1]
            f = amp[k]
            fe, fo = f[:, :HALF], f[:, HALF:]
            chi_r, chi_i = inverse(spec[k, m, 0] * jnp.concatenate([fe, fe], 1), spec[k, m, 1] * jnp.concatenate([fo, fo], 1), tab)
            contrib[k, 0] += pr * chi_r + pi * chi_i
            contrib[k, 1] += pr * chi_i - pi * chi_r
            qr = o_r * chi_r + o_i * chi_i
            qi = o_r * chi_i - o_i * chi_r
            gr = qr if gr is None else gr + qr
            gi = qi if gi is None else gi + qi
        pgm[m, pl.ds(0, W), :] = gr
        pgm[m, pl.ds(W, W), :] = gi

    def swap_copy(s):
        return remote(pgm.at[s, :, other], first.at[s], asend.at[0, s], arecv.at[0, s], twin)

    def halving_copy(i, s, off, to):
        n = ROWS >> (i + 1)
        return remote(data.at[s, pl.ds(pl.multiple_of(off, 8), n), :], later.at[s, pl.ds(ROWS - (ROWS >> i), n), :], asend.at[1 + i, s], arecv.at[1 + i, s], to)

    def merge(s):
        data[s] = pgm[s, :, mine] + first[s]

    def begin(s, bit):
        halving_copy(0, s, (1 - bit[0]) * W, bit[1:]).start()

    def tick(tau, turned):
        backward(tau)

        @pl.when(tau > 0)
        def _():
            swap_copy(tau - 1).wait()
            merge(tau - 1)
            begin(tau - 1, turned[3])

        swap_copy(tau).start()
        return turned[1:] + turned[:1]

    lax.fori_loop(0, MODES, tick, tuple(bits))

    def place(c):
        for k in range(2):
            mid[c, pl.ds(k * W, W), :] = select_right(contrib[k, c], cols_to[k])
        for j in range(3):
            cols = pl.ds(j * W, W)
            grad[c, :, cols] = select_left(rows_to[...], mid[c, :, cols])

    place(0)
    swap_copy(MODES - 1).wait()
    merge(MODES - 1)
    begin(MODES - 1, bits[(MODES - 1) % 4])
    place(1)

    h_corner = [remote(grad.at[c, pl.ds(TILE, W), pl.ds(TILE, W)], add_c.at[c], hsend.at[4 + c], hrecv.at[4 + c], right) for c in range(2)]
    h_side = [remote(grad.at[i // 2, pl.ds(i % 2 * W, W), pl.ds(TILE, W)], add_r.at[i // 2, pl.ds(i % 2 * W, W), :], hsend.at[6 + i], hrecv.at[6 + i], right) for i in range(4)]
    h_direct = [remote(cut(grad, i, TILE), cut(add_l, i, 0), hsend.at[i], hrecv.at[i], below) for i in range(4)]
    h_hop = [remote(cut(grad, i, TILE), cut(hold_out, i, 0), qsend.at[i], qrecv.at[i], (out_row, swap)) for i in range(4)]
    h_on = [remote(cut(hold_out, i, 0), cut(add_l, i, 0), qsend.at[4 + i], hrecv.at[i], (4, swap)) for i in range(4)]
    out_down = both(down, jnp.logical_not(out_src))

    def send_down(i):
        @pl.when(out_src)
        def _():
            h_hop[i].start()

        @pl.when(out_down)
        def _():
            h_direct[i].start()

    def send_side(*which):
        @pl.when(rht)
        def _():
            for i in which:
                h_side[i].start()

    def pass_on(*which):
        @pl.when(out_relay)
        def _():
            for i in which:
                h_hop[i].wait_recv()
                h_on[i].start()

    def turn_corner(c):
        @pl.when(both(down, lft))
        def _():
            h_corner[c].wait_recv()
            grad[c, pl.ds(TILE, W), pl.ds(0, W)] += add_c[c]

        send_down(c)

    @pl.when(both(down, rht))
    def _():
        h_corner[0].start()
        h_corner[1].start()

    send_down(2)
    send_down(3)

    offs = [[bits[s % 4][0] * W] for s in range(MODES)]
    flying = [halving_copy(0, s, (1 - bits[s % 4][0]) * W, bits[s % 4][1:]) for s in range(MODES)]

    def halve(i):
        for s in range(MODES):
            n = ROWS >> i
            off = offs[s][-1]
            flying[s].wait()
            data[s, pl.ds(pl.multiple_of(off, 8), n), :] += later[s, pl.ds(ROWS - (ROWS >> (i - 1)), n), :]
            if i < 4:
                g, to = bits[(s + i) % 4][0], bits[(s + i) % 4][1:]
                flying[s] = halving_copy(i, s, off + (1 - g) * (n // 2), to)
                flying[s].start()
                offs[s].append(off + g * (n // 2))
            else:
                ring[3, s] = data[s, pl.ds(pl.multiple_of(off, 8), n), :]
                flying[s] = remote(ring.at[3, s], ring.at[0, s], asend.at[5, s], arecv.at[5, s], y_next)
                flying[s].start()

    def around(i):
        for s in range(MODES):
            flying[s].wait()
            flying[s] = remote(ring.at[i - 1, s], ring.at[i, s], asend.at[5 + i, s], arecv.at[5 + i, s], y_next)
            flying[s].start()

    def widen(i):
        n = ROWS >> (i + 1)
        for s in range(MODES):
            flying[s].wait()
            off = pl.multiple_of(offs[s][i], 8)
            if i == 3:
                gath[s, pl.ds(off, n), :] = ((ring[(3 - y) % 4, s] + ring[(4 - y) % 4, s]) + (ring[(5 - y) % 4, s] + ring[(6 - y) % 4, s]))
            here = gath.at[s, pl.ds(off, n), :]
            flying[s] = remote(here, here, asend.at[11 - i, s], arecv.at[11 - i, s], bits[(s + i) % 4][1:])
            flying[s].start()

    halve(1)
    halve(2)
    pass_on(2)
    halve(3)
    turn_corner(0)
    pass_on(3)
    halve(4)
    send_side(0, 1)
    turn_corner(1)
    around(1)
    send_side(2)
    around(2)
    send_side(3)
    widen(3)
    pass_on(0)
    widen(2)
    pass_on(1)
    widen(1)
    widen(0)
    last = []
    for s in range(MODES):
        flying[s].wait()
        for c in range(2):
            here, there = gath.at[s, pl.ds(c * W, W), :], total.at[c, s, :, mine]
            last += [remote(here, there, asend.at[12 + c, s], arecv.at[12 + c, s], twin), pltpu.make_async_copy(here, there, osem.at[c, s])]
            last[-2].start()
            last[-1].start()

    @pl.when(lft)
    def _():
        for i in range(4):
            h_side[i].wait_recv()
        grad[:, pl.ds(0, TILE), pl.ds(0, W)] += add_r[...]

    @pl.when(up)
    def _():
        for c in h_direct:
            c.wait_recv()
        grad[:, pl.ds(0, W), pl.ds(0, TILE)] += add_l[...]

    result = pltpu.make_async_copy(grad.at[:, pl.ds(0, TILE), pl.ds(0, TILE)], own, lsem.at[0])
    result.start()

    @pl.when(in_src)
    def _():
        for c in in_hop:
            c.wait_send()

    @pl.when(in_up)
    def _():
        for c in in_direct:
            c.wait_send()

    @pl.when(in_relay)
    def _():
        for c in in_on:
            c.wait_send()

    @pl.when(lft)
    def _():
        side.wait_send()

    @pl.when(both(down, lft))
    def _():
        corner.wait_send()

    @pl.when(both(down, rht))
    def _():
        for c in h_corner:
            c.wait_send()

    @pl.when(rht)
    def _():
        for c in h_side:
            c.wait_send()

    @pl.when(out_src)
    def _():
        for c in h_hop:
            c.wait_send()

    @pl.when(out_down)
    def _():
        for c in h_direct:
            c.wait_send()

    @pl.when(out_relay)
    def _():
        for c in h_on:
            c.wait_send()

    for c in last:
        c.wait()
    result.wait()


def shards(object_field, probe, intensity, row_offset, col_offset, live):
    smem = pl.BlockSpec(memory_space=pltpu.SMEM)
    hbm = pl.BlockSpec(memory_space=pl.ANY)
    dma = pltpu.SemaphoreType.DMA
    half = pltpu.VMEM((MODES, ROWS, HALF), F32)
    object_grad, probe_grad = pl.pallas_call(
        main_kernel,
        out_shape=(
            jax.ShapeDtypeStruct((2, TILE, TILE), F32),
            jax.ShapeDtypeStruct((2, MODES, W, W), F32),
        ),
        in_specs=[smem, smem, smem, hbm, hbm, hbm, hbm, hbm],
        out_specs=(hbm, hbm),
        scratch_shapes=[
            pltpu.VMEM((2, EXT, EXT), F32),
            pltpu.VMEM((2, EXT, EXT), F32),
            pltpu.VMEM((2, 2 * W, EXT), F32),
            pltpu.VMEM((2 * W, EXT), BF),
            pltpu.VMEM((2, EXT, W), BF),
            pltpu.VMEM((EXT, 2 * W), BF),
            pltpu.VMEM((2, W, EXT), BF),
            pltpu.VMEM((2, 2, W, W), F32),
            pltpu.VMEM((2, MODES, 2, W, W), F32),
            pltpu.VMEM((2, 2, W, W), F32),
            pltpu.VMEM((2, W, W), F32),
            pltpu.VMEM((2, MODES, W, W), F32),
            pltpu.VMEM((2, W, W), F32),
            pltpu.VMEM((8, W, W), BF),
            pltpu.VMEM((2, W, W), BF),
            pltpu.VMEM((MODES, ROWS, W), F32),
            half, half, half, half,
            pltpu.VMEM((4, MODES, ROWS // 16, HALF), F32),
            pltpu.VMEM((2, W, TILE), F32),
            pltpu.VMEM((2, W, TILE), F32),
            pltpu.VMEM((2, W, W), F32),
            pltpu.VMEM((2, TILE, W), F32),
            pltpu.VMEM((2, W, TILE), F32),
            dma((5,)), dma((STAGES + 1, MODES)), dma((STAGES + 1, MODES)), dma((2, MODES)),
            dma((6,)), dma((6,)), dma((8,)), dma((4,)), dma((10,)), dma((10,)), dma((8,)), dma((4,)),
        ],
        compiler_params=pltpu.CompilerParams(collective_id=0, has_side_effects=True, vmem_limit_bytes=62 * 1024 * 1024),
        name="ptycho",
    )(row_offset, col_offset, live, object_field, probe, intensity, jnp.asarray(tables()), jnp.asarray(column_order()))
    return (object_grad, probe_grad)


def solution(mesh):
    in_specs = (
        P(None, "row", "col"),
        P(),
        P(("row", "col"), None, None),
        P(("row", "col")),
        P(("row", "col")),
        P(("row", "col")),
    )
    out_specs = (P(None, "row", "col"), P())
    return jax.shard_map(shards, mesh=mesh, in_specs=in_specs, out_specs=out_specs, check_vma=False)
```

time: 300 us -> 127 us (0.42)
  waiting for transfers between devices: 228 us -> 0 us
  Pallas kernels: 35.3 us -> 120 us
  between operations: 14.1 us -> 0.65 us
  starting transfers between devices: 10.1 us -> 0 us
  local copies, waits for them, and re-layouts: 8.73 us -> 5.25 us
  other arithmetic: 3.09 us -> 0 us
    psum x1 -> x0, waiting for transfers between devices: 154 us -> none  [shards(): probe_grad = lax.psum(partial_probe, ('row', 'col'))]
    pallas_call x1, Pallas kernels: 35.3 us -> 120 us  [shards(): pl.pallas_call(main_kernel, out_shape=(jax.ShapeDtypeStruct((2, TILE, TIL...]
    ppermute x4 -> x0, waiting for transfers between devices: 74.3 us -> none  [along(): return lax.ppermute(array, axis, pairs)]
    ppermute x4 -> x0, starting transfers between devices: 10 us -> none  [along(): return lax.ppermute(array, axis, pairs)]
  transfers between devices with their start and end apart: 5 -> 0, of which waited for: 5 -> 0; matrix products, arithmetic and copies ran while one was open for 2% -> 0% of each run, Pallas kernels for 0% -> 0%
where the time goes in v3:
time: 127 us; the launch traced here: 126 us
  Pallas kernels  120 us (94%)
  local copies, waits for them, and re-layouts  5.25 us (4%)
    pallas_call x1, Pallas kernels, shards(): pl.pallas_call(main_kernel, out_shape=(jax.ShapeDtypeStruct((2, TILE, TIL...  120 us
    unnamed x4, local copies, waits for them, and re-layouts  5.25 us

profile of v3, /device:TPU:1, one launch (start us, length us, event | category | flops | bytes accessed | tf_op | source)
XLA Modules:
  0.0 125.5 jit_solution(2488388844120427413)
XLA Ops:
  0.6 119.6 %ptycho.1 = (f32[2,512,512]{2,1,0:T(8,128)}, f32[2,8,256,256]{3,2,1,0:T(8,128)}) custom-call(s32[2]{0:T(128)} %top_ref.1, s32[2]{0:T(128)} %col_ref.1, s32[2]{0:T(128)} %live_ref.1, f32[2,512,512]{2,1,0:T(8,128)} %obj.1, f32[2,8,256,256]{3,2,1,0:T(8,128)} %probe_hbm.1, f32[2,256,256]{2,1,0:T(8,128)} %int_hbm.1, bf16[8,256,256]{2,1,0:T(8,128)(2,1)} %constant.4.clone.tab_hbm, ...), custom_call_target="tpu_custom_call" | custom-call | tf_op jit(solution)/shard_map/ptycho/pallas_call | solution.py:550
  120.2 0.0 copy-start
  120.2 3.2 %copy.12 = f32[2,512,512]{2,1,0:T(8,128)} copy(f32[2,512,512]{2,1,0:T(8,128)} %get-tuple-element.4) | data formatting | bytes 4194304
  123.5 0.0 copy-done
  123.5 2.0 %copy.13 = f32[2,8,256,256]{3,2,1,0:T(8,128)} copy(f32[2,8,256,256]{3,2,1,0:T(8,128)S(1)} %copy-done) | data formatting | bytes 8388608
Async XLA Ops:
  120.2 3.2 %copy-start = (f32[2,8,256,256]{3,2,1,0:T(8,128)S(1)}, f32[2,8,256,256]{3,2,1,0:T(8,128)}, u32[]{:S(2)}) copy-start(f32[2,8,256,256]{3,2,1,0:T(8,128)} %get-tuple-element.5) | copy-start | bytes 12582916

commit v4 on v3

--- a/solution.py
+++ b/solution.py
@@ -109,7 +109,7 @@
 N_ROW, N_COL = 8, 16
 ROWS = 2 * W
 STAGES = 13
-RELAY_IN, RELAY_OUT = 1, -1
+OUT_STEPS = (0, -1)
 
 
 def remote(src, dst, send, recv, to):
@@ -148,14 +148,13 @@
 
 
 def relay_roles(row, col, source, step):
-    odd, z_lo = col % 2 == 1, col // 8
-    target = 7 - source
-    y = source % 4
-    first = (source // 4 * 2 + step) % 4
-    second = (source // 4 * 2 + 1 + step) % 4
-    relay_row = (first // 2 * 4 + y) * (1 - z_lo) + (second // 2 * 4 + y) * z_lo
-    is_relay = both(odd, jnp.logical_or(both(row == first // 2 * 4 + y, z_lo == 1), both(row == second // 2 * 4 + y, z_lo == 0)))
-    return both(row == source, odd), both(row == target, odd), is_relay, relay_row
+    core, z_lo, y = col % 2, col // 8, source % 4
+    move = step[0] * (1 - core) + step[1] * core
+    first = (source // 4 * 2 + 4 + move) % 4 // 2 * 4 + y
+    second = (source // 4 * 2 + 5 + move) % 4 // 2 * 4 + y
+    used = move != 0
+    is_relay = jnp.logical_or(both(row == first, z_lo == 1), both(row == second, z_lo == 0))
+    return both(used, row == source), both(used, row == 7 - source), both(used, is_relay), first * (1 - z_lo) + second * z_lo
 
 
 def main_kernel(top_ref, col_ref, live_ref, obj, probe_hbm, int_hbm, tab_hbm, perm_hbm, own, total,
@@ -165,8 +164,8 @@
     row, col = lax.axis_index("row"), lax.axis_index("col")
     bits, core, twin, y, y_next, y_prev = hypercube(row, col)
     up, down, lft, rht = row > 0, row < N_ROW - 1, col > 0, col < N_COL - 1
-    in_src, in_dst, in_relay, in_row = relay_roles(row, col, 4, RELAY_IN)
-    out_src, out_dst, out_relay, out_row = relay_roles(row, col, 3, RELAY_OUT)
+    in_src, in_dst, in_relay, in_row = relay_roles(row, col, 4, (0, 1))
+    out_src, out_dst, out_relay, out_row = relay_roles(row, col, 3, OUT_STEPS)
     swap = col + 8 - 16 * (col // 8)
     yes = row >= 0
     no_down, no_rht = jnp.logical_not(down), jnp.logical_not(rht)
@@ -300,7 +299,7 @@
             amp[k] += jnp.concatenate([fe2[:, :HALF] + fe2[:, HALF:], fo2[:, :HALF] + fo2[:, HALF:]], 1)
         return carry
 
-    lax.fori_loop(0, MODES, forward, 0)
+    lax.fori_loop(0, MODES, forward, 0, unroll=2)
     for k in range(2):
         alive = live_ref[k].astype(F32)
         amp[k] = (1.0 - inten[k] / jnp.sqrt(amp[k] + 0.25)) * alive
@@ -402,13 +401,14 @@
 
         send_down(c)
 
-    @pl.when(both(down, rht))
-    def _():
-        h_corner[0].start()
-        h_corner[1].start()
+    def send_corner(c):
+        @pl.when(both(down, rht))
+        def _():
+            h_corner[c].start()
 
     send_down(2)
     send_down(3)
+    send_corner(0)
 
     offs = [[bits[s % 4][0] * W] for s in range(MODES)]
     flying = [halving_copy(0, s, (1 - bits[s % 4][0]) * W, bits[s % 4][1:]) for s in range(MODES)]
@@ -445,34 +445,43 @@
             here = gath.at[s, pl.ds(off, n), :]
             flying[s] = remote(here, here, asend.at[11 - i, s], arecv.at[11 - i, s], bits[(s + i) % 4][1:])
             flying[s].start()
+            if i == 0:
+                hand_over(s, 0)
+
+    last = []
+
+    def hand_over(s, second):
+        c = 1 - bits[s % 4][0] if second else bits[s % 4][0]
+        here, there = gath.at[s, pl.ds(pl.multiple_of(c * W, W), W), :], total.at[c, s, :, mine]
+        pair = [remote(here, there, asend.at[12 + second, s], arecv.at[12 + second, s], twin), pltpu.make_async_copy(here, there, osem.at[second, s])]
+        for d in pair:
+            d.start()
+        last.extend(pair)
 
     halve(1)
     halve(2)
+    send_corner(1)
+    halve(3)
     pass_on(2)
-    halve(3)
+    halve(4)
     turn_corner(0)
+    send_side(0)
+    around(1)
+    turn_corner(1)
     pass_on(3)
-    halve(4)
-    send_side(0, 1)
-    turn_corner(1)
-    around(1)
+    send_side(1)
+    around(2)
     send_side(2)
-    around(2)
+    pass_on(0)
+    widen(3)
+    pass_on(1)
     send_side(3)
-    widen(3)
-    pass_on(0)
     widen(2)
-    pass_on(1)
     widen(1)
     widen(0)
-    last = []
     for s in range(MODES):
         flying[s].wait()
-        for c in range(2):
-            here, there = gath.at[s, pl.ds(c * W, W), :], total.at[c, s, :, mine]
-            last += [remote(here, there, asend.at[12 + c, s], arecv.at[12 + c, s], twin), pltpu.make_async_copy(here, there, osem.at[c, s])]
-            last[-2].start()
-            last[-1].start()
+        hand_over(s, 1)
 
     @pl.when(lft)
     def _():

time: 127 us -> 125 us (0.984)
  no operation moved by 1% of the time
where the time goes in v4:
time: 125 us
  Pallas kernels  119 us (95%)
  local copies, waits for them, and re-layouts  5.25 us (4%)
    pallas_call x1, Pallas kernels, shards(): pl.pallas_call(main_kernel, out_shape=(jax.ShapeDtypeStruct((2, TILE, TIL...  119 us
    unnamed x4, local copies, waits for them, and re-layouts  5.25 us

profile of v4, /device:TPU:1, one launch (start us, length us, event | category | flops | bytes accessed | tf_op | source)
XLA Modules:
  0.0 124.6 jit_solution(12654601139403537940)
XLA Ops:
  0.6 118.7 %ptycho.1 = (f32[2,512,512]{2,1,0:T(8,128)}, f32[2,8,256,256]{3,2,1,0:T(8,128)}) custom-call(s32[2]{0:T(128)} %top_ref.1, s32[2]{0:T(128)} %col_ref.1, s32[2]{0:T(128)} %live_ref.1, f32[2,512,512]{2,1,0:T(8,128)} %obj.1, f32[2,8,256,256]{3,2,1,0:T(8,128)} %probe_hbm.1, f32[2,256,256]{2,1,0:T(8,128)} %int_hbm.1, bf16[8,256,256]{2,1,0:T(8,128)(2,1)} %constant.4.clone.tab_hbm, ...), custom_call_target="tpu_custom_call" | custom-call | tf_op jit(solution)/shard_map/ptycho/pallas_call | solution.py:559
  119.3 0.0 copy-start
  119.3 3.2 %copy.12 = f32[2,512,512]{2,1,0:T(8,128)} copy(f32[2,512,512]{2,1,0:T(8,128)} %get-tuple-element.4) | data formatting | bytes 4194304
  122.5 0.0 copy-done
  122.6 2.0 %copy.13 = f32[2,8,256,256]{3,2,1,0:T(8,128)} copy(f32[2,8,256,256]{3,2,1,0:T(8,128)S(1)} %copy-done) | data formatting | bytes 8388608
Async XLA Ops:
  119.3 3.2 %copy-start = (f32[2,8,256,256]{3,2,1,0:T(8,128)S(1)}, f32[2,8,256,256]{3,2,1,0:T(8,128)}, u32[]{:S(2)}) copy-start(f32[2,8,256,256]{3,2,1,0:T(8,128)} %get-tuple-element.5) | copy-start | bytes 12582916

commit v5 on v4

--- a/solution.py
+++ b/solution.py
@@ -362,59 +362,11 @@
     swap_copy(MODES - 1).wait()
     merge(MODES - 1)
     begin(MODES - 1, bits[(MODES - 1) % 4])
-    place(1)
-
-    h_corner = [remote(grad.at[c, pl.ds(TILE, W), pl.ds(TILE, W)], add_c.at[c], hsend.at[4 + c], hrecv.at[4 + c], right) for c in range(2)]
-    h_side = [remote(grad.at[i // 2, pl.ds(i % 2 * W, W), pl.ds(TILE, W)], add_r.at[i // 2, pl.ds(i % 2 * W, W), :], hsend.at[6 + i], hrecv.at[6 + i], right) for i in range(4)]
-    h_direct = [remote(cut(grad, i, TILE), cut(add_l, i, 0), hsend.at[i], hrecv.at[i], below) for i in range(4)]
-    h_hop = [remote(cut(grad, i, TILE), cut(hold_out, i, 0), qsend.at[i], qrecv.at[i], (out_row, swap)) for i in range(4)]
-    h_on = [remote(cut(hold_out, i, 0), cut(add_l, i, 0), qsend.at[4 + i], hrecv.at[i], (4, swap)) for i in range(4)]
-    out_down = both(down, jnp.logical_not(out_src))
-
-    def send_down(i):
-        @pl.when(out_src)
-        def _():
-            h_hop[i].start()
-
-        @pl.when(out_down)
-        def _():
-            h_direct[i].start()
-
-    def send_side(*which):
-        @pl.when(rht)
-        def _():
-            for i in which:
-                h_side[i].start()
-
-    def pass_on(*which):
-        @pl.when(out_relay)
-        def _():
-            for i in which:
-                h_hop[i].wait_recv()
-                h_on[i].start()
-
-    def turn_corner(c):
-        @pl.when(both(down, lft))
-        def _():
-            h_corner[c].wait_recv()
-            grad[c, pl.ds(TILE, W), pl.ds(0, W)] += add_c[c]
-
-        send_down(c)
-
-    def send_corner(c):
-        @pl.when(both(down, rht))
-        def _():
-            h_corner[c].start()
-
-    send_down(2)
-    send_down(3)
-    send_corner(0)
-
     offs = [[bits[s % 4][0] * W] for s in range(MODES)]
     flying = [halving_copy(0, s, (1 - bits[s % 4][0]) * W, bits[s % 4][1:]) for s in range(MODES)]
 
-    def halve(i):
-        for s in range(MODES):
+    def halve(i, streams=range(MODES)):
+        for s in streams:
             n = ROWS >> i
             off = offs[s][-1]
             flying[s].wait()
@@ -429,6 +381,56 @@
                 flying[s] = remote(ring.at[3, s], ring.at[0, s], asend.at[5, s], arecv.at[5, s], y_next)
                 flying[s].start()
 
+    halve(1, range(MODES - 1))
+    place(1)
+
+    h_corner = [remote(grad.at[c, pl.ds(TILE, W), pl.ds(TILE, W)], add_c.at[c], hsend.at[4 + c], hrecv.at[4 + c], right) for c in range(2)]
+    h_side = [remote(grad.at[i // 2, pl.ds(i % 2 * W, W), pl.ds(TILE, W)], add_r.at[i // 2, pl.ds(i % 2 * W, W), :], hsend.at[6 + i], hrecv.at[6 + i], right) for i in range(4)]
+    h_direct = [remote(cut(grad, i, TILE), cut(add_l, i, 0), hsend.at[i], hrecv.at[i], below) for i in range(4)]
+    h_hop = [remote(cut(grad, i, TILE), cut(hold_out, i, 0), qsend.at[i], qrecv.at[i], (out_row, swap)) for i in range(4)]
+    h_on = [remote(cut(hold_out, i, 0), cut(add_l, i, 0), qsend.at[4 + i], hrecv.at[i], (4, swap)) for i in range(4)]
+    out_down = both(down, jnp.logical_not(out_src))
+
+    def send_down(i):
+        @pl.when(out_src)
+        def _():
+            h_hop[i].start()
+
+        @pl.when(out_down)
+        def _():
+            h_direct[i].start()
+
+    def send_side(*which):
+        @pl.when(rht)
+        def _():
+            for i in which:
+                h_side[i].start()
+
+    def pass_on(*which):
+        @pl.when(out_relay)
+        def _():
+            for i in which:
+                h_hop[i].wait_recv()
+                h_on[i].start()
+
+    def turn_corner(c):
+        @pl.when(both(down, lft))
+        def _():
+            h_corner[c].wait_recv()
+            grad[c, pl.ds(TILE, W), pl.ds(0, W)] += add_c[c]
+
+        send_down(c)
+
+    def send_corner(c):
+        @pl.when(both(down, rht))
+        def _():
+            h_corner[c].start()
+
+    send_down(2)
+    send_down(3)
+    send_corner(0)
+
+
     def around(i):
         for s in range(MODES):
             flying[s].wait()
@@ -458,7 +460,7 @@
             d.start()
         last.extend(pair)
 
-    halve(1)
+    halve(1, [MODES - 1])
     halve(2)
     send_corner(1)
     halve(3)

time: 125 us -> 135 us (1.080)
  Pallas kernels: 119 us -> 128 us
    pallas_call x1, Pallas kernels: 119 us -> 128 us  [shards(): pl.pallas_call(main_kernel, out_shape=(jax.ShapeDtypeStruct((2, TILE, TIL...]
where the time goes in v5:
time: 135 us; the launch traced here: 134 us
  Pallas kernels  128 us (95%)
  local copies, waits for them, and re-layouts  5.25 us (4%)
    pallas_call x1, Pallas kernels, shards(): pl.pallas_call(main_kernel, out_shape=(jax.ShapeDtypeStruct((2, TILE, TIL...  128 us
    unnamed x4, local copies, waits for them, and re-layouts  5.25 us

profile of v5, /device:TPU:1, one launch (start us, length us, event | category | flops | bytes accessed | tf_op | source)
XLA Modules:
  0.0 133.8 jit_solution(14114576810824194805)
XLA Ops:
  0.6 127.9 %ptycho.1 = (f32[2,512,512]{2,1,0:T(8,128)}, f32[2,8,256,256]{3,2,1,0:T(8,128)}) custom-call(s32[2]{0:T(128)} %top_ref.1, s32[2]{0:T(128)} %col_ref.1, s32[2]{0:T(128)} %live_ref.1, f32[2,512,512]{2,1,0:T(8,128)} %obj.1, f32[2,8,256,256]{3,2,1,0:T(8,128)} %probe_hbm.1, f32[2,256,256]{2,1,0:T(8,128)} %int_hbm.1, bf16[8,256,256]{2,1,0:T(8,128)(2,1)} %constant.4.clone.tab_hbm, ...), custom_call_target="tpu_custom_call" | custom-call | tf_op jit(solution)/shard_map/ptycho/pallas_call | solution.py:561
  128.6 0.0 copy-start
  128.6 3.2 %copy.12 = f32[2,512,512]{2,1,0:T(8,128)} copy(f32[2,512,512]{2,1,0:T(8,128)} %get-tuple-element.4) | data formatting | bytes 4194304
  131.8 0.0 copy-done
  131.8 2.0 %copy.13 = f32[2,8,256,256]{3,2,1,0:T(8,128)} copy(f32[2,8,256,256]{3,2,1,0:T(8,128)S(1)} %copy-done) | data formatting | bytes 8388608
Async XLA Ops:
  128.6 3.2 %copy-start = (f32[2,8,256,256]{3,2,1,0:T(8,128)S(1)}, f32[2,8,256,256]{3,2,1,0:T(8,128)}, u32[]{:S(2)}) copy-start(f32[2,8,256,256]{3,2,1,0:T(8,128)} %get-tuple-element.5) | copy-start | bytes 12582916
